TPU v7x, 128 devices: a whole 4x4x4 slice. The times are simulated.
128 devices in a mesh: ctx: 32 (over z, x, core), head: 4 (over y).
Axes of the slice: x: 4, y: 4, z: 4, core: 2. Of those that a mesh axis runs over, the one named last changes fastest.
Arguments:
- queries: bfloat16 [16384, 2048], P('ctx', 'head'), may hold values from -6 to 6
- key_rows: bfloat16 [16384, 2048], P('ctx', 'head'), may hold values from -6 to 6
- value_rows: bfloat16 [16384, 2048], P('ctx', 'head'), may hold values from -6 to 6
- targets: bfloat16 [16384, 512], P('ctx'), may hold values from -2.5 to 2.5
- readout: bfloat16 [512, 4096], P(None, 'head'), may hold values from -0.25 to 0.25
- retain: float32 [32, 16], P('ctx', 'head'), may hold values from 0.3 to 1
- learn_rate: float32 [32, 16], P('ctx', 'head'), may hold values from 0.01 to 0.1
- allowed: int32 [32, 2], replicated, may hold values 0 or 1
- positions: int32 [32, 128], P('ctx'), may hold values from 0 to 511, as said below
- grad_out: bfloat16 [16384, 2048], P('ctx', 'head'), may hold values from -6 to 6
Outputs:
- grad_queries: float32 [16384, 2048], P('ctx', 'head')
- grad_keys: float32 [16384, 2048], P('ctx', 'head')
- grad_values: float32 [16384, 2048], P('ctx', 'head')
- grad_targets: float32 [16384, 512], P('ctx', 'head')
- grad_readout: float32 [512, 4096], P('ctx', 'head')
Inputs may be any that keep to these rules, and one draw needn't show every extreme that they name: The 128 positions of a segment are distinct, ascending, and include 0 and 511.
All inputs are finite; a program needn't handle non-finite values.
Results may differ from a plain program's by a relative error of at most 0.0081.
Values may be sent and summed in bfloat16 or wider, within the bound.
A program may use at most 192 MiB of HBM per device.

v0:
```python
from functools import reduce

import jax
import jax.numpy as jnp
from jax import lax
from jax.sharding import PartitionSpec as P

masked_score = -1e30
highest = lax.Precision.HIGHEST


def entering(value, axis, join, neutral, backward):
    count, mine = (lax.axis_size(axis), lax.axis_index(axis))
    pieces = jax.tree.map(lambda part: lax.all_gather(part, axis), value)
    if backward:
        pieces = jax.tree.map(lambda part: part[::-1], pieces)
        mine = count - 1 - mine
    subtotal = jax.tree.map(
        lambda part, zero: jnp.full_like(part, 0) + jnp.asarray(zero, part.dtype), value, neutral
    )

    def turn(position, subtotal):
        longer = join(subtotal, jax.tree.map(lambda part: part[position], pieces))
        return jax.tree.map(lambda new, old: jnp.where(position < mine, new, old), longer, subtotal)

    return lax.fori_loop(0, count - 1, turn, subtotal)


def shifted_2(value, axis, steps):
    count = lax.axis_size(axis)
    leading, last = (max(0, -steps), min(count, count - steps))
    return lax.ppermute(value, axis, [(source, source + steps) for source in range(leading, last)])


def compose(earlier_map, later_map):
    linear_part = jnp.einsum("hab,hbc->hac", later_map[0], earlier_map[0], precision=highest)
    shift_part = (
        jnp.einsum("hab,hbf->haf", later_map[0], earlier_map[1], precision=highest) + later_map[1]
    )
    return (linear_part, shift_part)


def score_block(left_rows, right_rows, score_scale):
    return (
        lax.dot_general(
            left_rows, right_rows, (((1,), (1,)), ((), ())), preferred_element_type=jnp.float32
        )
        * score_scale
    )


def gated_scores(left_rows, right_rows, usable, score_scale):
    return jnp.where(usable, score_block(left_rows, right_rows, score_scale), masked_score)


def scores_grad(cotangent, values_tile, probs_tile, row_delta):
    grad_probs = lax.dot_general(
        cotangent, values_tile, (((1,), (1,)), ((), ())), preferred_element_type=jnp.float32
    )
    return (probs_tile * (grad_probs - row_delta)).astype(jnp.bfloat16)


def block_all(
    queries_tile, cotangent, keys_tile, values_tile, probs_tile, probs_low, row_delta, score_scale
):
    grad_scores = scores_grad(cotangent, values_tile, probs_tile, row_delta)
    grad_rows = jnp.dot(grad_scores, keys_tile, preferred_element_type=jnp.float32) * score_scale
    grad_cols = (
        lax.dot_general(
            grad_scores, queries_tile, (((0,), (0,)), ((), ())), preferred_element_type=jnp.float32
        )
        * score_scale
    )
    grad_vals = lax.dot_general(
        probs_low, cotangent, (((0,), (0,)), ((), ())), preferred_element_type=jnp.float32
    )
    return (grad_rows, grad_cols, grad_vals)


def far_all(
    queries_tile, cotangent, keys_tile, values_tile, probs_tile, probs_low, row_delta, score_scale
):
    return block_all(
        queries_tile,
        cotangent,
        keys_tile,
        values_tile,
        probs_tile,
        probs_low,
        row_delta,
        score_scale,
    )


def on_device(
    queries,
    key_rows,
    value_rows,
    targets,
    readout,
    retain,
    learn_rate,
    allowed,
    positions,
    grad_out,
):
    seg_len = queries.shape[0]
    local_heads = retain.shape[1]
    head_width = queries.shape[1] // local_heads
    mem_rows = positions.shape[1]
    block_reach = allowed.shape[1]
    segment = lax.axis_index("ctx")
    score_scale = head_width ** (-0.5)
    key_heads = key_rows.reshape(seg_len, local_heads, head_width)
    key_gram = jnp.einsum("sha,shb->hab", key_heads, key_heads, preferred_element_type=jnp.float32)
    identity_block = jnp.eye(head_width, dtype=jnp.float32)
    decay_map = (
        retain[0][:, None, None] * identity_block
        - (learn_rate[0] / seg_len)[:, None, None] * key_gram
    )
    write_map = (
        jnp.einsum("sha,sf->haf", key_heads, targets, preferred_element_type=jnp.float32) / seg_len
    )
    neutral = (jnp.broadcast_to(identity_block, decay_map.shape), jnp.zeros_like(write_map))
    memory_in = entering((decay_map, write_map), "ctx", compose, neutral, False)[1]
    pick_rows = positions[0]
    picked = (
        jnp.take(queries, pick_rows, axis=0)
        .astype(jnp.float32)
        .reshape(mem_rows, local_heads, head_width)
    )
    partial_read = jnp.einsum("nha,haf->nf", picked, memory_in, precision=highest)
    hidden_read = lax.psum(partial_read, "head").astype(jnp.bfloat16)
    memory_tokens = jnp.dot(hidden_read, readout, preferred_element_type=jnp.float32).reshape(
        mem_rows, local_heads, 2, head_width
    )
    memory_keys = memory_tokens[:, :, 0].astype(jnp.bfloat16)
    memory_values = memory_tokens[:, :, 1].astype(jnp.bfloat16)
    remote = []
    for offset in range(1, block_reach + 1):
        shifted = shifted_2((key_rows, value_rows), "ctx", offset)
        usable = (allowed[segment, offset - 1] == 1) & (segment >= offset)
        remote.append((shifted[0], shifted[1], usable))
    causal = lax.broadcasted_iota(jnp.int32, (seg_len, seg_len), 0) >= lax.broadcasted_iota(
        jnp.int32, (seg_len, seg_len), 1
    )
    rows_list, keys_own, values_own = ([], [], [])
    mem_key_grads, mem_value_grads = ([], [])
    far_keys = [[] for offset in range(block_reach)]
    far_values = [[] for offset in range(block_reach)]
    max_list, total_list, delta_list = ([], [], [])
    for head_index in range(local_heads):
        columns = slice(head_index * head_width, (head_index + 1) * head_width)
        queries_tile = queries[:, columns]
        cotangent = grad_out[:, columns]
        key_collection = [memory_keys[:, head_index], key_rows[:, columns]] + [
            remote_item[0][:, columns] for remote_item in remote
        ]
        values_list = [memory_values[:, head_index], value_rows[:, columns]] + [
            remote_item[1][:, columns] for remote_item in remote
        ]
        score_list = [
            score_block(queries_tile, key_collection[0], score_scale),
            jnp.where(
                causal, score_block(queries_tile, key_collection[1], score_scale), masked_score
            ),
        ]
        score_list = score_list + [
            gated_scores(
                queries_tile, key_collection[2 + tile_index], remote[tile_index][2], score_scale
            )
            for tile_index in range(block_reach)
        ]
        row_max = reduce(
            jnp.maximum, [jnp.max(score_tile, axis=1, keepdims=True) for score_tile in score_list]
        )
        exp_tiles = [jnp.exp(score_tile - row_max) for score_tile in score_list]
        row_total = reduce(
            jnp.add, [jnp.sum(exp_tile, axis=1, keepdims=True) for exp_tile in exp_tiles]
        )
        probs_list = [exp_tile / row_total for exp_tile in exp_tiles]
        probs_lows = [probs_tile.astype(jnp.bfloat16) for probs_tile in probs_list]
        attended = reduce(
            jnp.add,
            [
                jnp.dot(low_tile, value_tile, preferred_element_type=jnp.float32)
                for low_tile, value_tile in zip(probs_lows, values_list)
            ],
        )
        row_delta = jnp.sum(cotangent.astype(jnp.float32) * attended, axis=1, keepdims=True)
        mem_grads = block_all(
            queries_tile,
            cotangent,
            key_collection[0],
            values_list[0],
            probs_list[0],
            probs_lows[0],
            row_delta,
            score_scale,
        )
        own_grads = block_all(
            queries_tile,
            cotangent,
            key_collection[1],
            values_list[1],
            probs_list[1],
            probs_lows[1],
            row_delta,
            score_scale,
        )
        grad_rows = mem_grads[0] + own_grads[0]
        for tile_index in range(block_reach):
            far_grads = far_all(
                queries_tile,
                cotangent,
                key_collection[2 + tile_index],
                values_list[2 + tile_index],
                probs_list[2 + tile_index],
                probs_lows[2 + tile_index],
                row_delta,
                score_scale,
            )
            grad_rows = grad_rows + far_grads[0]
            far_keys[tile_index].append(far_grads[1])
            far_values[tile_index].append(far_grads[2])
        rows_list.append(grad_rows)
        keys_own.append(own_grads[1])
        values_own.append(own_grads[2])
        mem_key_grads.append(mem_grads[1])
        mem_value_grads.append(mem_grads[2])
        max_list.append(row_max)
        total_list.append(row_total)
        delta_list.append(row_delta)
    grad_queries = jnp.concatenate(rows_list, axis=1)
    key_total = jnp.concatenate(keys_own, axis=1)
    value_total = jnp.concatenate(values_own, axis=1)
    for offset in range(1, block_reach + 1):
        returned = shifted_2(
            (
                jnp.concatenate(far_keys[offset - 1], axis=1),
                jnp.concatenate(far_values[offset - 1], axis=1),
            ),
            "ctx",
            -offset,
        )
        key_total = key_total + returned[0]
        value_total = value_total + returned[1]
    grad_memory = jnp.stack(
        [jnp.stack(mem_key_grads, axis=1), jnp.stack(mem_value_grads, axis=1)], axis=2
    )
    grad_memory = grad_memory.reshape(mem_rows, local_heads * 2 * head_width).astype(jnp.bfloat16)
    readout_term = lax.dot_general(
        hidden_read, grad_memory, (((0,), (0,)), ((), ())), preferred_element_type=jnp.float32
    )
    grad_readout = lax.psum_scatter(readout_term, "ctx", scatter_dimension=0, tiled=True)
    hidden_term = lax.dot_general(
        grad_memory, readout, (((1,), (1,)), ((), ())), preferred_element_type=jnp.float32
    )
    grad_hidden = lax.psum(hidden_term, "head")
    grad_picked = jnp.einsum("nf,haf->nha", grad_hidden, memory_in, precision=highest).reshape(
        mem_rows, local_heads * head_width
    )
    grad_state = jnp.einsum("nha,nf->haf", picked, grad_hidden, precision=highest)
    grad_queries = grad_queries + jnp.zeros_like(grad_queries).at[pick_rows].add(grad_picked)
    flipped = jnp.swapaxes(decay_map, 1, 2)
    grad_after = entering((flipped, grad_state), "ctx", compose, neutral, True)[1]
    grad_decay = jnp.einsum("haf,hbf->hab", grad_after, memory_in, precision=highest)
    symmetric = grad_decay + jnp.swapaxes(grad_decay, 1, 2)
    keys_wide = key_heads.astype(jnp.float32)
    key_memory = (
        jnp.einsum("sf,haf->sha", targets.astype(jnp.float32), grad_after, precision=highest)
        / seg_len
    )
    key_memory = key_memory - (learn_rate[0] / seg_len)[None, :, None] * jnp.einsum(
        "sha,hab->shb", keys_wide, symmetric, precision=highest
    )
    key_total = key_total + key_memory.reshape(seg_len, local_heads * head_width)
    target_term = jnp.einsum("sha,haf->sf", keys_wide, grad_after, precision=highest) / seg_len
    grad_targets = lax.psum_scatter(target_term, "head", scatter_dimension=1, tiled=True)
    return (grad_queries, key_total, value_total, grad_targets, grad_readout)


def solution(mesh):
    return jax.shard_map(
        on_device,
        mesh=mesh,
        in_specs=(
            P("ctx", "head"),
            P("ctx", "head"),
            P("ctx", "head"),
            P("ctx", None),
            P(None, "head"),
            P("ctx", "head"),
            P("ctx", "head"),
            P(),
            P("ctx", None),
            P("ctx", "head"),
        ),
        out_specs=(
            P("ctx", "head"),
            P("ctx", "head"),
            P("ctx", "head"),
            P("ctx", "head"),
            P("ctx", "head"),
        ),
        check_vma=False,
    )
```

profile of v0, /device:TPU:0, one launch (start us, length us, event | category | flops | bytes accessed | tf_op | source)
XLA Modules:
  0.0 802.2 jit_solution(9045116034539921850)
XLA Ops:
  15.3 2.5 convolution_multiply_fusion.14
  17.8 4.3 collective-permute-start.3
  24.4 3.1 collective-permute-start.1
  27.5 3.7 collective-permute-start
  45.8 2.7 fusion.313
  48.5 2.7 fusion.317
  51.3 2.7 fusion.311
  60.6 2.8 fusion.310
  63.4 2.8 fusion.314
  66.2 2.7 fusion.318
  68.9 2.7 fusion.322
  71.6 21.3 %all-gather.9.cloned.1.call-done = f32[128,128,128]{2,1,0:T(8,128)} async-done(((f32[4,128,128]{2,1,0:T(8,128)}), f32[128,128,128]{2,1,0:T(8,128)}) %all-gather.9.cloned.1.call-update) | async-done | bytes 8388624 | tf_op jit(solution)/shard_map/all_gather | solution.py:14
  92.9 115.6 %all-gather.11.cloned.1.call-done = f32[128,128,512]{2,1,0:T(8,128)} async-done(((f32[4,128,512]{2,1,0:T(8,128)}), f32[128,128,512]{2,1,0:T(8,128)}) %all-gather.11.cloned.1.call-update) | async-done | bytes 33554448 | tf_op jit(solution)/shard_map/all_gather | solution.py:14
  208.5 78.0 %while.28 = (s32[]{:T(128)}, f32[4,128,512]{2,1,0:T(8,128)S(1)}, s32[]{:T(128)}, f32[32,4,128,128]{3,2,1,0:T(8,128)}, f32[32,4,128,512]{3,2,1,0:T(8,128)}, /*index=5*/s32[]{:T(128)}, s32[]{:T(128)}) while((s32[]{:T(128)}, f32[4,128,512]{2,1,0:T(8,128)S(1)}, s32[]{:T(128)}, f32[32,4,128,128]{3,2,1,0:T(8,128)}, ...), condition=%wide.region_1.2_spmd.clone, body=%wide.region_0.1_spmd.clone.sunk | while | flops 403701760 | bytes 6556263 | solution.py:26
  287.8 21.1 %all-reduce.4 = bf16[128,512]{1,0:T(8,128)(2,1)S(1)} all-reduce(f32[128,512]{1,0:T(8,128)} %convolution_bitcast_fusion.1), channel_id=1, replica_groups=mesh['ctx'=32,'head'=4] {'head'}, use_global_device_ids=true, to_apply=%region_2.3 | all-reduce | flops 65536 | bytes 393216 | tf_op jit(solution)/shard_map/psum | solution.py:133
  313.8 2.4 fusion.105
  341.4 37.8 %all-reduce.3.cloned.1.call-done = f32[128,512]{1,0:T(8,128)} async-done(((f32[128,512]{1,0:T(8,128)}), f32[128,512]{1,0:T(8,128)}) %all-reduce.3.cloned.1.call-update) | async-done | bytes 262160 | tf_op jit(solution)/shard_map/psum | solution.py:259
  379.1 2.6 fusion.142
  382.3 52.2 %all-gather.13.cloned.1.call-done = f32[128,128,128]{2,1,0:T(8,128)} async-done(((f32[4,128,128]{2,1,0:T(8,128)}), f32[128,128,128]{2,1,0:T(8,128)}) %all-gather.13.cloned.1.call-update) | async-done | bytes 8388624 | tf_op jit(solution)/shard_map/all_gather | solution.py:14
  434.6 7.9 rev.6
  474.5 2.5 copy.111
  496.5 84.6 %all-gather.15.cloned.1.call-done = f32[128,128,512]{2,1,0:T(8,128)} async-done(((f32[4,128,512]{2,1,0:T(8,128)}), f32[128,128,512]{2,1,0:T(8,128)}) %all-gather.15.cloned.1.call-update) | async-done | bytes 33554448 | tf_op jit(solution)/shard_map/all_gather | solution.py:14
  581.2 23.4 %rev.7 = f32[32,4,128,512]{3,2,1,0:T(8,128)} reverse(f32[32,4,128,512]{3,2,1,0:T(8,128)} %bitcast.227), dimensions={0} | reverse | bytes 67108864 | tf_op jit(solution)/shard_map/rev | solution.py:16
  604.6 78.1 %while.29 = (s32[]{:T(128)}, f32[4,128,512]{2,1,0:T(8,128)S(1)}, s32[]{:T(128)}, f32[32,4,128,128]{3,2,1,0:T(8,128)}, f32[32,4,128,512]{3,2,1,0:T(8,128)}, /*index=5*/s32[]{:T(128)}, s32[]{:T(128)}) while((s32[]{:T(128)}, f32[4,128,512]{2,1,0:T(8,128)S(1)}, s32[]{:T(128)}, f32[32,4,128,128]{3,2,1,0:T(8,128)}, ...), condition=%wide.region_42.43_spmd.clone, body=%wide.region_41.42_spmd.clone.sunk | while | flops 403701760 | bytes 6556263 | solution.py:26
  607.2 2.4 fusion.421
  612.2 2.4 fusion.421
  682.8 4.0 fusion.42
  721.2 3.7 scatter_fusion
  724.9 3.1 fusion.97
  728.0 2.6 copy.120
  736.5 3.5 collective-permute-done.5
  745.4 49.8 %reduce-scatter.5.cloned.1.call-done = f32[16,1024]{1,0:T(8,128)} async-done(((f32[512,1024]{1,0:T(8,128)}), f32[16,1024]{1,0:T(8,128)}) %reduce-scatter.5.cloned.1.call-update) | async-done | bytes 65552 | tf_op jit(solution)/shard_map/reduce_scatter | solution.py:255
  (514 shorter events, 306.4 us)
Async XLA Ops:
  7.2 301.8 %copy-start = (bf16[512,1024]{1,0:T(8,128)(2,1)S(1)}, bf16[512,1024]{1,0:T(8,128)(2,1)}, u32[]{:S(2)}) copy-start(bf16[512,1024]{1,0:T(8,128)(2,1)} %param.18) | copy-start | bytes 3145732
  7.2 26.2 %copy-start.8 = (bf16[512,512]{1,0:T(8,128)(2,1)S(1)}, bf16[512,512]{1,0:T(8,128)(2,1)}, u32[]{:S(2)}) copy-start(bf16[512,512]{1,0:T(8,128)(2,1)} %param.15) | copy-start | bytes 1572868
  7.2 25.3 %copy-start.5 = (bf16[512,512]{1,0:T(8,128)(2,1)S(1)}, bf16[512,512]{1,0:T(8,128)(2,1)}, u32[]{:S(2)}) copy-start(bf16[512,512]{1,0:T(8,128)(2,1)} %param.23) | copy-start | bytes 1572868
  7.2 26.1 %copy-start.2 = (bf16[512,512]{1,0:T(8,128)(2,1)S(1)}, bf16[512,512]{1,0:T(8,128)(2,1)}, u32[]{:S(2)}) copy-start(bf16[512,512]{1,0:T(8,128)(2,1)} %param.14) | copy-start | bytes 1572868
  7.2 29.9 %copy-start.102 = (s32[32,2]{0,1:T(2,128)S(1)}, s32[32,2]{0,1:T(2,128)}, u32[]{:S(2)}) copy-start(s32[32,2]{0,1:T(2,128)} %param.21) | copy-start | bytes 772
  7.2 85.7 %all-gather.9.cloned.1.call-start = ((), (), s32[]{:S(2)}) async-start(), calls=%async_computation.5 | async-start | bytes 8650752 | tf_op jit(solution)/shard_map/all_gather | solution.py:14
  8.1 23.1 %copy-start.100 = (f32[4]{0:T(128)}, f32[4]{0:T(128)S(1)}, u32[]{:S(2)}) copy-start(f32[4]{0:T(128)S(1)} %multiply_bitcast_fusion) | copy-start | bytes 52
  15.2 193.2 %all-gather.11.cloned.1.call-start = ((), (), s32[]{:S(2)}) async-start(), calls=%async_computation.6 | async-start | bytes 34603008 | tf_op jit(solution)/shard_map/all_gather | solution.py:14
  17.8 361.3 %all-reduce.3.cloned.1.call-start = ((), (), s32[]{:S(2)}) async-start(), calls=%async_computation.2 | async-start | bytes 524288 | tf_op jit(solution)/shard_map/psum | solution.py:259
  17.8 305.4 %collective-permute-start.3 = (bf16[512,512]{1,0:T(8,128)(2,1)}, bf16[512,512]{1,0:T(8,128)(2,1)}, u32[]{:S(2)}, u32[]{:S(2)}) collective-permute-start(bf16[512,512]{1,0:T(8,128)(2,1)} %param.16), channel_id=1, source_target_pairs={{0,8},{4,12},{8,16},{12,20},{16,24},{20,28},{24,32},{28,36},{32,40... | collective-permute-start | bytes 1572872 | tf_op jit(solution)/shard_map/ppermute | solution.py:32
  22.2 303.4 %collective-permute-start.2 = (bf16[512,512]{1,0:T(8,128)(2,1)}, bf16[512,512]{1,0:T(8,128)(2,1)}, u32[]{:S(2)}, u32[]{:S(2)}) collective-permute-start(bf16[512,512]{1,0:T(8,128)(2,1)} %param.16), channel_id=1, source_target_pairs={{0,4},{4,8},{8,12},{12,16},{16,20},{20,24},{24,28},{28,32},{32,36}... | collective-permute-start | bytes 1572872 | tf_op jit(solution)/shard_map/ppermute | solution.py:32
  24.4 36.2 %collective-permute-start.1 = (bf16[512,512]{1,0:T(8,128)(2,1)}, bf16[512,512]{1,0:T(8,128)(2,1)}, u32[]{:S(2)}, u32[]{:S(2)}) collective-permute-start(bf16[512,512]{1,0:T(8,128)(2,1)} %param.15), channel_id=1, source_target_pairs={{0,8},{4,12},{8,16},{12,20},{16,24},{20,28},{24,32},{28,36},{32,40... | collective-permute-start | bytes 1572872 | tf_op jit(solution)/shard_map/ppermute | solution.py:32
  27.5 23.8 %collective-permute-start = (bf16[512,512]{1,0:T(8,128)(2,1)}, bf16[512,512]{1,0:T(8,128)(2,1)}, u32[]{:S(2)}, u32[]{:S(2)}) collective-permute-start(bf16[512,512]{1,0:T(8,128)(2,1)} %param.15), channel_id=1, source_target_pairs={{0,4},{4,8},{8,12},{12,16},{16,20},{20,24},{24,28},{28,32},{32,36}... | collective-permute-start | bytes 1572872 | tf_op jit(solution)/shard_map/ppermute | solution.py:32
  32.5 254.0 %copy-start.96 = (pred[128]{0:T(512)(128)(4,1)}, pred[128]{0:T(512)(128)(4,1)S(1)}, u32[]{:S(2)}) copy-start(pred[128]{0:T(512)(128)(4,1)S(1)} %compare_and_fusion) | copy-start | bytes 388
  40.0 246.6 %copy-start.63 = (bf16[128,512]{0,1:T(8,128)(2,1)}, bf16[128,512]{0,1:T(8,128)(2,1)S(1)}, u32[]{:S(2)}) copy-start(bf16[128,512]{0,1:T(8,128)(2,1)S(1)} %copy.137) | copy-start | bytes 393220
  316.2 21.0 %copy-start.78 = (f32[512]{0:T(512)}, f32[512]{0:T(512)S(1)}, u32[]{:S(2)}) copy-start(f32[512]{0:T(512)S(1)} %add_add_fusion.2) | copy-start | bytes 6148
  318.0 15.5 %copy-start.80 = (f32[512]{0:T(512)}, f32[512]{0:T(512)S(1)}, u32[]{:S(2)}) copy-start(f32[512]{0:T(512)S(1)} %add_add_fusion.3) | copy-start | bytes 6148
  339.5 95.1 %all-gather.13.cloned.1.call-start = ((), (), s32[]{:S(2)}) async-start(), calls=%async_computation.7 | async-start | bytes 8650752 | tf_op jit(solution)/shard_map/all_gather | solution.py:14
  341.3 239.8 %all-gather.15.cloned.1.call-start = ((), (), s32[]{:S(2)}) async-start(), calls=%async_computation.8 | async-start | bytes 34603008 | tf_op jit(solution)/shard_map/all_gather | solution.py:14
  381.7 361.8 %reduce-scatter.3.cloned.1.call-start = ((), (), s32[]{:S(2)}) async-start(), calls=%async_computation.3 | async-start | bytes 1310720 | tf_op jit(solution)/shard_map/reduce_scatter | solution.py:279
  477.1 16.4 %copy-start.27 = (bf16[512,512]{0,1:T(8,128)(2,1)S(1)}, bf16[512,512]{0,1:T(8,128)(2,1)}, u32[]{:S(2)}) copy-start(bf16[512,512]{0,1:T(8,128)(2,1)} %copy-done.26) | copy-start | bytes 1572868
  477.1 17.5 %copy-start.29 = (bf16[512,512]{0,1:T(8,128)(2,1)S(1)}, bf16[512,512]{0,1:T(8,128)(2,1)}, u32[]{:S(2)}) copy-start(bf16[512,512]{0,1:T(8,128)(2,1)} %copy-done.28) | copy-start | bytes 1572868
  477.1 18.5 %copy-start.31 = (bf16[512,512]{0,1:T(8,128)(2,1)S(1)}, bf16[512,512]{0,1:T(8,128)(2,1)}, u32[]{:S(2)}) copy-start(bf16[512,512]{0,1:T(8,128)(2,1)} %copy-done.30) | copy-start | bytes 1572868
  484.2 252.3 %collective-permute-start.4 = (f32[512,512]{0,1:T(8,128)}, f32[512,512]{0,1:T(8,128)}, u32[]{:S(2)}, u32[]{:S(2)}) collective-permute-start(f32[512,512]{0,1:T(8,128)} %pad_maximum_fusion.1), channel_id=1, source_target_pairs={{4,0},{8,4},{12,8},{16,12},{20,16},{24,20},{28,24},{32,28},{36,32}... | collective-permute-start | bytes 3145736 | tf_op jit(solution)/shard_map/ppermute | solution.py:32
  491.0 233.9 %collective-permute-start.7 = (f32[512,512]{0,1:T(8,128)}, f32[512,512]{0,1:T(8,128)}, u32[]{:S(2)}, u32[]{:S(2)}) collective-permute-start(f32[512,512]{0,1:T(8,128)} %pad_maximum_fusion.4), channel_id=1, source_target_pairs={{8,0},{12,4},{16,8},{20,12},{24,16},{28,20},{32,24},{36,28},{40,32... | collective-permute-start | bytes 3145736 | tf_op jit(solution)/shard_map/ppermute | solution.py:32
  682.7 16.0 %copy-start.4 = (bf16[512,512]{1,0:T(8,128)(2,1)S(1)}, bf16[512,512]{1,0:T(8,128)(2,1)}, u32[]{:S(2)}) copy-start(bf16[512,512]{1,0:T(8,128)(2,1)} %param.14) | copy-start | bytes 1572868
  686.7 108.4 %reduce-scatter.5.cloned.1.call-start = ((), (), s32[]{:S(2)}) async-start(), calls=%async_computation.4 | async-start | bytes 2162688 | tf_op jit(solution)/shard_map/reduce_scatter | solution.py:255
  689.1 35.8 %collective-permute-start.6 = (f32[512,512]{0,1:T(8,128)}, f32[512,512]{0,1:T(8,128)}, u32[]{:S(2)}, u32[]{:S(2)}) collective-permute-start(f32[512,512]{0,1:T(8,128)} %pad_maximum_fusion.3), channel_id=1, source_target_pairs={{4,0},{8,4},{12,8},{16,12},{20,16},{24,20},{28,24},{32,28},{36,32}... | collective-permute-start | bytes 3145736 | tf_op jit(solution)/shard_map/ppermute | solution.py:32
  696.7 24.5 %copy-start.98 = (s32[128]{0:T(128)S(1)}, s32[128]{0:T(128)}, u32[]{:S(2)}) copy-start(s32[128]{0:T(128)} %copy-done.97) | copy-start | bytes 1540
  706.8 18.1 %copy-start.64 = (f32[512,128]{0,1:T(8,128)S(1)}, f32[512,128]{0,1:T(8,128)}, u32[]{:S(2)}) copy-start(f32[512,128]{0,1:T(8,128)} %fusion.279) | copy-start | bytes 786436
  711.6 28.4 %collective-permute-start.5 = (f32[512,512]{0,1:T(8,128)}, f32[512,512]{0,1:T(8,128)}, u32[]{:S(2)}, u32[]{:S(2)}) collective-permute-start(f32[512,512]{0,1:T(8,128)} %pad_maximum_fusion.2), channel_id=1, source_target_pairs={{8,0},{12,4},{16,8},{20,12},{24,16},{28,20},{32,24},{36,28},{40,32... | collective-permute-start | bytes 3145736 | tf_op jit(solution)/shard_map/ppermute | solution.py:32
  728.0 67.1 %copy-start.1 = (bf16[512,1024]{1,0:T(8,128)(2,1)S(1)}, bf16[512,1024]{1,0:T(8,128)(2,1)}, u32[]{:S(2)}) copy-start(bf16[512,1024]{1,0:T(8,128)(2,1)} %param.18) | copy-start | bytes 3145732
  (86 other events, 599.6 us)
Sparse Core Ops, SparseCore 0:
  15.4 77.4 all-gather.8
  95.1 113.3 all-gather.10
  339.6 39.4 all-reduce.2
  381.2 53.2 all-gather.12
  436.7 144.4 all-gather.14
  686.9 25.3 reduce-scatter.2
  716.3 78.7 reduce-scatter.4
where the time goes:
time: 812 us; the launch traced here: 802 us
  waiting for transfers between devices  365 us (45%)
  matrix products  281 us (35%)
  local copies, waits for them, and re-layouts  66.5 us (8%)
  other arithmetic  29.6 us (4%)
  blocking collectives  21.1 us (3%)
  starting transfers between devices  19.5 us (2%)
  between operations  17.7 us (2%)
    all_gather x4, waiting for transfers between devices, entering(): pieces = jax.tree.map(lambda part: lax.all_gather(part, axis), value)  274 us
    dot_general x62, matrix products, compose(): jnp.einsum('hab,hbf->haf', later_map[0], earlier_map[1], precision=highest)  150 us
    reduce_scatter x1, waiting for transfers between devices, on_device(): lax.psum_scatter(readout_term, 'ctx', scatter_dimension=0, tiled=True)  49.8 us
    psum x1, waiting for transfers between devices, on_device(): grad_hidden = lax.psum(hidden_term, 'head')  37.8 us
    rev x2, local copies, waits for them, and re-layouts, entering(): pieces = jax.tree.map(lambda part: part[::-1], pieces)  31.3 us
    dot_general x16, matrix products, score_block(): lax.dot_general(left_rows, right_rows, (((1,), (1,)), ((), ())), preferre...  30.4 us
    dot_general x16, matrix products, block_all(): lax.dot_general(grad_scores, queries_tile, (((0,), (0,)), ((), ())), pref...  22.2 us
    psum x1, blocking collectives, on_device(): hidden_read = lax.psum(partial_read, 'head').astype(jnp.bfloat16)  21.1 us
  transfers between devices with their start and end apart: 15, of which 7 were waited for; matrix products, arithmetic and copies ran while one was open for 44% of the time, Pallas kernels for 0%

commit v1 on v0

v1 whole, which is shorter than its diff:
```python
import functools

import jax
import jax.numpy as jnp
from jax import lax
from jax.experimental import pallas as pl
from jax.experimental.pallas import tpu as pltpu
from jax.sharding import PartitionSpec as P

MESH = pl.DeviceIdType.MESH
BF = jnp.bfloat16
F32 = jnp.float32
NEG = -1e30
SEGS, HEADS, DK, FH, SEG, NM, PEERS = 32, 4, 128, 512, 512, 128, 4
WIDE = HEADS * DK
COLS = SEGS // HEADS
PIECE = FH // COLS
ROWS_R = 16
VM = pl.BlockSpec(memory_space=pltpu.VMEM)
SM = pl.BlockSpec(memory_space=pltpu.SMEM)
ANY = pl.BlockSpec(memory_space=pl.ANY)
LIMIT = 60 * 1024 * 1024


def nn(a, b):
    return lax.dot_general(a, b, (((1,), (0,)), ((), ())), preferred_element_type=F32)


def nt(a, b):
    return lax.dot_general(a, b, (((1,), (1,)), ((), ())), preferred_element_type=F32)


def tn(a, b):
    return lax.dot_general(a, b, (((0,), (0,)), ((), ())), preferred_element_type=F32)


def head(h):
    return slice(h * DK, (h + 1) * DK)


def prep_kernel(retain, rate, q, k, z, pos, er, bt, picked):
    onehot = (
        lax.broadcasted_iota(jnp.int32, (SEG, NM), 0) == pos[...]
    ).astype(F32).astype(BF)
    picked[...] = tn(onehot, q[...]).astype(BF)
    row = lax.broadcasted_iota(jnp.int32, (ROWS_R, DK), 0)
    for h in range(HEADS):
        kh = k[:, head(h)]
        er[h, 0:DK, :] = (tn(kh, kh) * (rate[0, h] / SEG)).astype(BF)
        whole = jnp.full((ROWS_R, DK), retain[0, h], F32)
        first = whole.astype(BF).astype(F32)
        second = (whole - first).astype(BF).astype(F32)
        third = whole - first - second
        er[h, DK:, :] = jnp.where(
            row == 0, first, jnp.where(row == 1, second, jnp.where(row == 2, third, 0.0))
        ).astype(BF)
        bt[h * COLS : (h + 1) * COLS] = (tn(z[...], kh) * (1.0 / SEG)).reshape(COLS, PIECE, DK)


def remote(src, dst, send, recv, where):
    return pltpu.make_async_remote_copy(
        src_ref=src, dst_ref=dst, send_sem=send, recv_sem=recv, device_id=where, device_id_type=MESH
    )


def enter(me, my):
    barrier = pltpu.get_barrier_semaphore()

    @pl.loop(1, SEGS)
    def _(d):
        pl.semaphore_signal(
            barrier, inc=1, device_id={"ctx": lax.rem(me + d, SEGS)}, device_id_type=MESH
        )

    for d in range(1, PEERS):
        pl.semaphore_signal(
            barrier, inc=1, device_id={"head": lax.rem(my + d, PEERS)}, device_id_type=MESH
        )
    pl.semaphore_wait(barrier, SEGS - 1 + PEERS - 1)


def retained(er_all, t):
    return jnp.sum(er_all[t, DK:, :].astype(F32), axis=0, keepdims=True)


def sum_over_heads(block, mine, landing, gathered, my, s_y, r_y):
    for d in range(PEERS):
        mine[d] = block(lax.rem(my + d, PEERS))

    def scatter(d):
        to = lax.rem(my + d, PEERS)
        return remote(mine.at[d], landing.at[d], s_y.at[d], r_y.at[d], {"head": to})

    def gather(d):
        to = lax.rem(my + d, PEERS)
        return remote(gathered.at[my], gathered.at[my], s_y.at[PEERS + d], r_y.at[PEERS + d], {"head": to})

    def started():
        for d in range(1, PEERS):
            scatter(d).start()

    def summed():
        total = mine[0]
        for d in range(1, PEERS):
            scatter(d).wait_recv()
            total = total + landing[d]
        gathered[my] = total.astype(BF)
        for d in range(1, PEERS):
            gather(d).start()

    def finished():
        for d in range(1, PEERS):
            src = lax.rem(my + PEERS - d, PEERS)
            remote(
                gathered.at[src], gathered.at[src], s_y.at[PEERS + d], r_y.at[PEERS + d], {"head": src}
            ).wait_recv()
        for d in range(1, PEERS):
            scatter(d).wait_send()
            gather(d).wait_send()
        return jnp.concatenate([gathered[j] for j in range(PEERS)], axis=1)

    return started, summed, finished


def forward_kernel(
    er, bt, kk, vv, qq, gg, picked, readout,
    er_out, mt_out, k1, v1, k2, v2, q1, g1, q2, g2, hid, tok,
    er_all, bt_all, outb, mt, mine_y, land_y, gath_y, part, state,
    s_er, r_er, s_bt, r_bt, s_m, r_m, s_halo, r_halo, s_y, r_y, loc,
):
    me, my = lax.axis_index("ctx"), lax.axis_index("head")
    mine = lax.div(me, COLS)
    core = lax.rem(me, 2)
    partner = me + 1 - 2 * core
    enter(me, my)

    def er_copy(to, src):
        return remote(er.at[lax.div(to, COLS)], er_all.at[src], s_er.at[to], r_er.at[src], {"ctx": to})

    def bt_copy(to, src):
        return remote(bt.at[to], bt_all.at[src], s_bt.at[to], r_bt.at[src], {"ctx": to})

    def m_copy(to, src):
        return remote(outb.at[to], mt.at[src], s_m.at[to], r_m.at[src], {"ctx": to})

    @pl.loop(1, SEGS)
    def _(d):
        to = lax.rem(me + d, SEGS)
        er_copy(to, me).start()
        bt_copy(to, me).start()

    def halo(src, dst, i, to):
        return remote(src, dst, s_halo.at[i], r_halo.at[i], {"ctx": to})

    after, before = lax.rem(me + 2, SEGS), lax.rem(me + SEGS - 2, SEGS)
    far = [
        halo(kk, k2, 0, after),
        halo(vv, v2, 1, after),
        halo(qq, q2, 2, before),
        halo(gg, g2, 3, before),
    ]
    keys_near = [halo(kk, k1, 4, partner), halo(vv, v1, 5, partner)]
    rows_near = [halo(qq, q1, 6, partner), halo(gg, g1, 7, partner)]
    keys_relay = [halo(k2, k1, 4, partner), halo(v2, v1, 5, partner)]
    rows_relay = [halo(q2, q1, 6, partner), halo(g2, g1, 7, partner)]
    for copy in far:
        copy.start()

    @pl.when(core == 0)
    def _():
        for copy in keys_near:
            copy.start()

    @pl.when(core == 1)
    def _():
        for copy in rows_near:
            copy.start()

    own_er = pltpu.make_async_copy(er.at[mine], er_all.at[me], loc.at[0])
    own_bt = pltpu.make_async_copy(bt.at[me], bt_all.at[me], loc.at[1])
    own_er.start()
    own_bt.start()
    own_er.wait()
    own_bt.wait()

    @pl.loop(1, SEGS)
    def _(d):
        src = lax.rem(me + SEGS - d, SEGS)
        er_copy(src, src).wait_recv()
        bt_copy(src, src).wait_recv()

    state[...] = jnp.zeros((PIECE, DK), F32)

    @pl.loop(0, SEGS)
    def _(t):
        old = state[...]
        outb[t] = old
        state[...] = retained(er_all, t) * old - nn(old.astype(BF), er_all[t, 0:DK, :]) + bt_all[t]

        @pl.when((t > 0) & (t - 1 != me))
        def _():
            m_copy(t - 1, me).start()

    @pl.when(me != SEGS - 1)
    def _():
        m_copy(SEGS - 1, me).start()

    own_m = pltpu.make_async_copy(outb.at[me], mt.at[me], loc.at[2])
    own_m.start()
    own_m.wait()

    @pl.loop(1, SEGS)
    def _(d):
        to = lax.rem(me + d, SEGS)
        er_copy(to, me).wait_send()
        bt_copy(to, me).wait_send()
        m_copy(to, me).wait_send()
        m_copy(to, to).wait_recv()

    for h in range(HEADS):
        m_h = mt[h * COLS : (h + 1) * COLS].reshape(FH, DK)
        high = m_h.astype(BF)
        low = (m_h - high.astype(F32)).astype(BF)
        mt_out[h * COLS : (h + 1) * COLS] = high.reshape(COLS, PIECE, DK)
        term = nt(picked[:, head(h)], high) + nt(picked[:, head(h)], low)
        for j in range(PEERS):
            if h == 0:
                part[j] = term[:, head(j)]
            else:
                part[j] += term[:, head(j)]
    started, summed, finished = sum_over_heads(lambda j: part[j], mine_y, land_y, gath_y, my, s_y, r_y)
    started()
    er_out[...] = er_all[...]
    summed()

    for copy in far:
        copy.wait_recv()

    @pl.when(core == 1)
    def _():
        for copy in keys_relay:
            copy.start()

    @pl.when(core == 0)
    def _():
        for copy in rows_relay:
            copy.start()

    low = finished()
    hid[...] = low
    tok[...] = nn(low, readout[...]).astype(BF)
    for copy in far:
        copy.wait_send()
    for copy in keys_near + rows_near:
        copy.wait()


def attention_kernel(allowed, q, g, k, v, k1, v1, k2, v2, tok, dq, dk, dv, gm, stats):
    scale = DK**-0.5
    segment = lax.axis_index("ctx")
    uses = [
        (allowed[segment, offset] == 1) & (segment > offset) for offset in range(2)
    ]
    q_t, g_t = q[...], g[...]
    causal = lax.broadcasted_iota(jnp.int32, (SEG, SEG), 0) >= lax.broadcasted_iota(
        jnp.int32, (SEG, SEG), 1
    )
    keys = [tok[:, 0:DK], k[...], k1[...], k2[...]]
    vals = [tok[:, DK:], v[...], v1[...], v2[...]]
    scores = [nt(q_t, key) for key in keys]
    scores[1] = jnp.where(causal, scores[1], NEG)
    scores[2] = jnp.where(uses[0], scores[2], NEG)
    scores[3] = jnp.where(uses[1], scores[3], NEG)
    top = functools.reduce(jnp.maximum, [jnp.max(s, axis=1, keepdims=True) for s in scores])
    exps = [jnp.exp((s - top) * scale) for s in scores]
    total = functools.reduce(jnp.add, [jnp.sum(e, axis=1, keepdims=True) for e in exps])
    inverse = 1.0 / total
    probs = [e * inverse for e in exps]
    lows = [p.astype(BF) for p in probs]
    attended = functools.reduce(jnp.add, [nn(p, value) for p, value in zip(lows, vals)])
    delta = jnp.sum(g_t.astype(F32) * attended, axis=1, keepdims=True)
    grads = [
        (p * (nt(g_t, value) - delta)).astype(BF) for p, value in zip(probs, vals)
    ]
    gm[:, 0:DK] = (tn(grads[0], q_t) * scale).astype(BF)
    gm[:, DK:] = tn(lows[0], g_t).astype(BF)
    dq[...] = functools.reduce(jnp.add, [nn(s, key) for s, key in zip(grads, keys)]) * scale
    dk[...] = tn(grads[1], q_t) * scale
    dv[...] = tn(lows[1], g_t)
    level = top * scale + jnp.log(total)
    lane = lax.broadcasted_iota(jnp.int32, (SEG, DK), 1)
    columns = jnp.where(
        lane == 0,
        jnp.where(uses[0], level, -NEG),
        jnp.where(lane == 1, jnp.where(uses[1], level, -NEG), delta),
    )
    stats[...] = columns.T[0:8, :]


def backward_kernel(
    rate, gm, readout, picked, hid, pos, stats, er_all_h, mt_h, kk_h, vv_h, zz_h, q1_h, g1_h, q2_h, g2_h,
    dq_h, dk_h, dv_h,
    out_q, out_k, out_v, out_z, out_r,
    er_all, mt, kk, vv, zz, q1, g1, q2, g2, dq, dk, dv,
    part, mine_y, land_y, gath_y, gsb, gs_all, gout, gt, rbuf, rall, tparts, st_in, state,
    s_gs, r_gs, s_g, r_g, s_r, r_r, s_y, r_y, s_t, r_t, s_st, r_st, loc, fetch,
):
    me, my = lax.axis_index("ctx"), lax.axis_index("head")
    scale = DK**-0.5
    fetched = [
        pltpu.make_async_copy(src, dst, fetch.at[i])
        for i, (src, dst) in enumerate(
            (
                (kk_h, kk), (vv_h, vv), (q1_h, q1), (g1_h, g1), (q2_h, q2), (g2_h, g2), (dk_h, dk), (dv_h, dv),
                (mt_h, mt), (dq_h, dq), (er_all_h, er_all), (zz_h, zz),
            )
        )
    ]
    for copy in fetched:
        copy.start()
    enter(me, my)

    def stat_copy(o):
        to = lax.rem(me + SEGS - o, SEGS)
        return remote(stats, st_in.at[o - 1], s_st.at[o - 1], r_st.at[o - 1], {"ctx": to})

    def gs_copy(to, src):
        return remote(gsb.at[to], gs_all.at[src], s_gs.at[to], r_gs.at[src], {"ctx": to})

    def g_copy(to, src):
        return remote(gout.at[to], gt.at[src], s_g.at[to], r_g.at[src], {"ctx": to})

    def r_copy(to, src):
        return remote(rbuf.at[to], rall.at[src], s_r.at[to], r_r.at[src], {"ctx": to})

    def far_tile(o, h):
        q_t, g_t = (q1, g1) if o == 1 else (q2, g2)
        q_t, g_t = q_t[:, head(h)], g_t[:, head(h)]
        level = st_in[o - 1, 8 * h + o - 1 : 8 * h + o, :]
        delta = st_in[o - 1, 8 * h + 2 : 8 * h + 3, :]
        probs = jnp.exp(nt(kk[:, head(h)], q_t) * scale - level)
        grads = probs * (nt(vv[:, head(h)], g_t) - delta)
        dv[:, head(h)] += nn(probs.astype(BF), g_t)
        dk[:, head(h)] += nn(grads.astype(BF), q_t) * scale

    term = nt(gm[...], readout[...])
    for j in range(PEERS):
        part[j] = term[:, head(j)]
    started, summed, finished = sum_over_heads(lambda j: part[j], mine_y, land_y, gath_y, my, s_y, r_y)
    started()
    for o in (1, 2):
        stat_copy(o).start()
    rbuf[...] = tn(hid[...], gm[...]).astype(BF).reshape(SEGS, FH // SEGS, 2 * WIDE)
    for copy in fetched[:8]:
        copy.wait()
    for o in (1, 2):
        stat_copy(o).wait()
    summed()
    far_tile(1, 0)
    far_tile(2, 0)
    gh = finished()

    for h in range(HEADS):
        gsb[h * COLS : (h + 1) * COLS] = (
            tn(gh, picked[:, head(h)]).astype(BF).reshape(COLS, PIECE, DK)
        )

    @pl.loop(1, SEGS)
    def _(d):
        gs_copy(lax.rem(me + d, SEGS), me).start()

    @pl.loop(1, SEGS)
    def _(d):
        r_copy(lax.rem(me + d, SEGS), me).start()

    own_gs = pltpu.make_async_copy(gsb.at[me], gs_all.at[me], loc.at[0])
    own_r = pltpu.make_async_copy(rbuf.at[me], rall.at[me], loc.at[1])
    own_gs.start()
    own_r.start()

    for h in range(1, HEADS):
        far_tile(1, h)
        far_tile(2, h)
    for copy in fetched[8:]:
        copy.wait()

    own_gs.wait()
    own_r.wait()

    @pl.loop(1, SEGS)
    def _(d):
        src = lax.rem(me + SEGS - d, SEGS)
        gs_copy(src, src).wait_recv()

    state[...] = jnp.zeros((PIECE, DK), F32)

    @pl.loop(0, SEGS)
    def _(i):
        t = SEGS - 1 - i
        old = state[...]
        low = old.astype(BF)
        gout[t] = low
        state[...] = retained(er_all, t) * old - nn(low, er_all[t, 0:DK, :]) + gs_all[t].astype(F32)

        @pl.when((i > 0) & (t + 1 != me))
        def _():
            g_copy(t + 1, me).start()

    @pl.when(me != 0)
    def _():
        g_copy(0, me).start()

    own_g = pltpu.make_async_copy(gout.at[me], gt.at[me], loc.at[2])
    own_g.start()

    onehot = (
        lax.broadcasted_iota(jnp.int32, (SEG, NM), 0) == pos[...]
    ).astype(F32).astype(BF)
    for h in range(HEADS):
        m_h = mt[h * COLS : (h + 1) * COLS].reshape(FH, DK)
        grad_picked = nn(gh, m_h).astype(BF)
        out_q[:, head(h)] = dq[:, head(h)] + nn(onehot, grad_picked)
    out_v[...] = dv[...]

    own_g.wait()

    @pl.loop(1, SEGS)
    def _(d):
        to = lax.rem(me + d, SEGS)
        gs_copy(to, me).wait_send()
        g_copy(to, me).wait_send()
        g_copy(to, to).wait_recv()

    term = jnp.zeros((SEG, FH), F32)
    for h in range(HEADS):
        g_h = gt[h * COLS : (h + 1) * COLS].reshape(FH, DK)
        term += nt(kk[:, head(h)], g_h)
    term = (term * (1.0 / SEG)).astype(BF)
    for j in range(PEERS):
        tparts[j] = term[:, head(j)]

    def t_copy(d):
        to = lax.rem(my + d, PEERS)
        return remote(tparts.at[to], tparts.at[PEERS + d], s_t.at[d], r_t.at[d], {"head": to})

    for d in range(1, PEERS):
        t_copy(d).start()

    for h in range(HEADS):
        g_h = gt[h * COLS : (h + 1) * COLS].reshape(FH, DK)
        m_h = mt[h * COLS : (h + 1) * COLS].reshape(FH, DK)
        both = (tn(g_h, m_h) + tn(m_h, g_h)).astype(BF)
        out_k[:, head(h)] = (
            dk[:, head(h)]
            + nn(zz[...], g_h) * (1.0 / SEG)
            - nn(kk[:, head(h)], both) * (rate[0, h] / SEG)
        )

    @pl.loop(1, SEGS)
    def _(d):
        to = lax.rem(me + d, SEGS)
        r_copy(to, me).wait_send()
        r_copy(to, to).wait_recv()

    out_r[...] = jnp.sum(rall[...].astype(F32), axis=0)

    for d in range(1, PEERS):
        t_copy(d).wait()
    grad = tparts[my].astype(F32)
    for d in range(1, PEERS):
        grad += tparts[PEERS + d].astype(F32)
    out_z[...] = grad


def shape(dims, kind):
    return jax.ShapeDtypeStruct(dims, kind)


def dma(*dims):
    return pltpu.SemaphoreType.DMA(dims)


def on_device(
    queries, key_rows, value_rows, targets, readout, retain, learn_rate, allowed, positions, grad_out
):
    block = (SEG, WIDE)
    er, bt, picked = pl.pallas_call(
        prep_kernel,
        out_shape=(
            shape((HEADS, DK + ROWS_R, DK), BF),
            shape((SEGS, PIECE, DK), F32),
            shape((NM, WIDE), BF),
        ),
        in_specs=[SM, SM, VM, VM, VM, VM],
        out_specs=(VM, VM, VM),
        name="prep",
    )(retain, learn_rate, queries, key_rows, targets, positions)

    sums = [
        pltpu.VMEM((PEERS, NM, FH // PEERS), F32),
        pltpu.VMEM((PEERS, NM, FH // PEERS), F32),
        pltpu.VMEM((PEERS, NM, FH // PEERS), BF),
    ]
    er_all, mt, k1, v1, k2, v2, q1, g1, q2, g2, hid, tok = pl.pallas_call(
        forward_kernel,
        out_shape=(
            shape((SEGS, DK + ROWS_R, DK), BF),
            shape((SEGS, PIECE, DK), BF),
        )
        + (shape(block, BF),) * 8
        + (
            shape((NM, FH), BF),
            shape((NM, 2 * WIDE), BF),
        ),
        in_specs=[VM, VM, ANY, ANY, ANY, ANY, VM, VM],
        out_specs=(VM, VM) + (ANY,) * 8 + (VM, VM),
        scratch_shapes=[
            pltpu.VMEM((SEGS, DK + ROWS_R, DK), BF),
            pltpu.VMEM((SEGS, PIECE, DK), F32),
            pltpu.VMEM((SEGS, PIECE, DK), F32),
            pltpu.VMEM((SEGS, PIECE, DK), F32),
        ]
        + sums
        + [
            pltpu.VMEM((PEERS, NM, FH // PEERS), F32),
            pltpu.VMEM((PIECE, DK), F32),
            dma(SEGS), dma(SEGS), dma(SEGS), dma(SEGS), dma(SEGS), dma(SEGS),
            dma(8), dma(8), dma(2 * PEERS), dma(2 * PEERS), dma(3),
        ],
        compiler_params=pltpu.CompilerParams(
            collective_id=0, has_side_effects=True, vmem_limit_bytes=LIMIT
        ),
        name="forward_scan",
    )(er, bt, key_rows, value_rows, queries, grad_out, picked, readout)

    one = pl.BlockSpec((SEG, DK), lambda h: (0, h))
    wide = pl.BlockSpec((NM, 2 * DK), lambda h: (0, h))
    dq, dk, dv, gm, stats = pl.pallas_call(
        attention_kernel,
        grid=(HEADS,),
        out_shape=(
            shape(block, F32),
            shape(block, F32),
            shape(block, F32),
            shape((NM, 2 * WIDE), BF),
            shape((8 * HEADS, SEG), F32),
        ),
        in_specs=[SM] + [one] * 8 + [wide],
        out_specs=(one,) * 3 + (wide, pl.BlockSpec((8, SEG), lambda h: (h, 0))),
        compiler_params=pltpu.CompilerParams(vmem_limit_bytes=LIMIT),
        name="attention",
    )(allowed, queries, grad_out, key_rows, value_rows, k1, v1, k2, v2, tok)

    return pl.pallas_call(
        backward_kernel,
        out_shape=(
            shape(block, F32),
            shape(block, F32),
            shape(block, F32),
            shape((SEG, FH // PEERS), F32),
            shape((FH // SEGS, 2 * WIDE), F32),
        ),
        in_specs=[SM] + [VM] * 6 + [ANY] * 12,
        out_specs=(VM,) * 5,
        scratch_shapes=[
            pltpu.VMEM((SEGS, DK + ROWS_R, DK), BF),
            pltpu.VMEM((SEGS, PIECE, DK), BF),
        ]
        + [pltpu.VMEM(block, BF)] * 7
        + [pltpu.VMEM(block, F32)] * 3
        + [pltpu.VMEM((PEERS, NM, FH // PEERS), F32)]
        + sums
        + [
            pltpu.VMEM((SEGS, PIECE, DK), BF),
            pltpu.VMEM((SEGS, PIECE, DK), BF),
            pltpu.VMEM((SEGS, PIECE, DK), BF),
            pltpu.VMEM((SEGS, PIECE, DK), BF),
            pltpu.VMEM((SEGS, FH // SEGS, 2 * WIDE), BF),
            pltpu.VMEM((SEGS, FH // SEGS, 2 * WIDE), BF),
            pltpu.VMEM((2 * PEERS, SEG, FH // PEERS), BF),
            pltpu.VMEM((2, 8 * HEADS, SEG), F32),
            pltpu.VMEM((PIECE, DK), F32),
            dma(SEGS), dma(SEGS), dma(SEGS), dma(SEGS), dma(SEGS), dma(SEGS),
            dma(2 * PEERS), dma(2 * PEERS), dma(PEERS), dma(PEERS), dma(2), dma(2), dma(3), dma(12),
        ],
        compiler_params=pltpu.CompilerParams(
            collective_id=1, has_side_effects=True, vmem_limit_bytes=LIMIT
        ),
        name="backward_scan",
    )(
        learn_rate, gm, readout, picked, hid, positions, stats, er_all, mt, key_rows, value_rows, targets,
        q1, g1, q2, g2, dq, dk, dv,
    )


def solution(mesh):
    return jax.shard_map(
        on_device,
        mesh=mesh,
        in_specs=(
            P("ctx", "head"),
            P("ctx", "head"),
            P("ctx", "head"),
            P("ctx", None),
            P(None, "head"),
            P("ctx", "head"),
            P("ctx", "head"),
            P(),
            P("ctx", None),
            P("ctx", "head"),
        ),
        out_specs=(P("ctx", "head"),) * 5,
        check_vma=False,
    )
```

time: 812 us -> 175 us (0.22); the launches traced: 802 us -> 175 us
  waiting for transfers between devices: 365 us -> 0 us
  matrix products: 281 us -> 0 us
  Pallas kernels: 0 us -> 166 us
  local copies, waits for them, and re-layouts: 66.5 us -> 7.74 us
  other arithmetic: 29.6 us -> 0 us
  blocking collectives: 21.1 us -> 0 us
  starting transfers between devices: 19.5 us -> 0 us
  between operations: 17.7 us -> 0.67 us
    dot_general x170 -> x0, matrix products: 281 us -> none  [the longest x62 150 us: compose(): jnp.einsum('hab,hbf->haf', later_map[0], earlier_map[1], precision=highest)]
    all_gather x4 -> x0, waiting for transfers between devices: 274 us -> none  [entering(): pieces = jax.tree.map(lambda part: lax.all_gather(part, axis), value)]
    pallas_call x0 -> x4, Pallas kernels: none -> 166 us  [the longest x1 88.2 us: on_device(): pl.pallas_call(forward_kernel, out_shape=(shape((SEGS, DK + ROWS_R, DK),...]
    reduce_scatter x2 -> x0, waiting for transfers between devices: 49.8 us -> none  [the longest x1 49.8 us: on_device(): lax.psum_scatter(readout_term, 'ctx', scatter_dimension=0, tiled=True)]
    psum x1 -> x0, waiting for transfers between devices: 37.8 us -> none  [on_device(): grad_hidden = lax.psum(hidden_term, 'head')]
    rev x2 -> x0, local copies, waits for them, and re-layouts: 31.3 us -> none  [entering(): pieces = jax.tree.map(lambda part: part[::-1], pieces)]
    psum x1 -> x0, blocking collectives: 21.1 us -> none  [on_device(): hidden_read = lax.psum(partial_read, 'head').astype(jnp.bfloat16)]
    ppermute x8 -> x0, starting transfers between devices: 18.7 us -> none  [shifted_2(): lax.ppermute(value, axis, [(source, source + steps) for source in range(l...]
  transfers between devices with their start and end apart: 15 -> 0, of which waited for: 7 -> 0; matrix products, arithmetic and copies ran while one was open for 44% -> 0% of each run, Pallas kernels for 0% -> 0%
where the time goes in v1:
time: 175 us
  Pallas kernels  166 us (95%)
  local copies, waits for them, and re-layouts  7.74 us (4%)
    pallas_call x1, Pallas kernels, on_device(): pl.pallas_call(forward_kernel, out_shape=(shape((SEGS, DK + ROWS_R, DK),...  88.2 us
    pallas_call x1, Pallas kernels, on_device(): pl.pallas_call(backward_kernel, out_shape=(shape(block, F32), shape(block...  59.4 us
    pallas_call x1, Pallas kernels, on_device(): pl.pallas_call(attention_kernel, grid=(HEADS,), out_shape=(shape(block, F...  15.4 us
    unnamed x14, local copies, waits for them, and re-layouts  7.74 us

profile of v1, /device:TPU:0, one launch (start us, length us, event | category | flops | bytes accessed | tf_op | source)
XLA Modules:
  0.0 174.8 jit_solution(15075583423203478105)
XLA Ops:
  0.6 1.4 copy.15.allowed
  2.0 3.3 %prep.1 = (bf16[4,144,128]{2,1,0:T(8,128)(2,1)}, f32[32,64,128]{2,1,0:T(8,128)}, bf16[128,512]{1,0:T(8,128)(2,1)}) custom-call(f32[1,4]{1,0:T(1,128)} %retain.1, f32[1,4]{1,0:T(1,128)} %rate.3, bf16[512,512]{1,0:T(8,128)(2,1)} %q.3, bf16[512,512]{1,0:T(8,128)(2,1)} %kk_h.1, bf16[512,512]{1,0:T(8,128)(2,1)} %zz_h.1, s32[1,128]{1,0:T(1,128)} %pos.3), custom_call_target="tpu_custom_call" | custom-call | tf_op jit(solution)/shard_map/prep/pallas_call | solution.py:487
  5.3 88.2 %forward_scan.1 = (bf16[32,144,128]{2,1,0:T(8,128)(2,1)}, bf16[32,64,128]{2,1,0:T(8,128)(2,1)}, bf16[512,512]{1,0:T(8,128)(2,1)}, bf16[512,512]{1,0:T(8,128)(2,1...) custom-call(bf16[4,144,128]{2,1,0:T(8,128)(2,1)} %get-tuple-element., ...), custom_call_target="tpu_custom_call" | custom-call | tf_op jit(solution)/shard_map/forward_scan/pallas_call | solution.py:504
  93.6 15.4 %attention.1 = (f32[512,512]{1,0:T(8,128)}, f32[512,512]{1,0:T(8,128)}, f32[512,512]{1,0:T(8,128)}, bf16[128,1024]{1,0:T(8,128)(2,1)}, f32[32,512]{1,0:T(8,128)}) custom-call(s32[32,2]{1,0:T(8,128)} %copy.15.allowed, bf16[512,512]{1,0:T(8,128)(2,1)} %q.3, bf16[512,512]{1,0:T(8,128)(2,1)} %g.1, bf16[512,512]{1,0:T(8,128)(2,1)} %kk_h.1, ...), custom_call_target="tpu_custom_call" | custom-call | tf_op jit(solution)/shard_map/attention/pallas_call | solution.py:538
  109.0 59.4 %backward_scan.1 = (f32[512,512]{1,0:T(8,128)}, f32[512,512]{1,0:T(8,128)}, f32[512,512]{1,0:T(8,128)}, f32[512,128]{1,0:T(8,128)}, f32[16,1024]{1,0:T(8,128)}) custom-call(f32[1,4]{1,0:T(1,128)} %rate.3, bf16[128,1024]{1,0:T(8,128)(2,1)} %get-tuple-element.33.gm, bf16[512,1024]{1,0:T(8,128)(2,1)} %readout.3, bf16[128,512]{1,0:T(8,128)(2,1)} %get-tuple-element.27.picked, ...), custom_call_target="tpu_custom_call" | custom-call | tf_op jit(solution)/shard_map/backward_scan/pallas_call | solution.py:554
  168.4 0.0 copy-start.1
  168.4 2.4 %copy.21 = f32[512,512]{1,0:T(8,128)} copy(f32[512,512]{1,0:T(8,128)} %get-tuple-element.50) | data formatting | bytes 2097152
  170.8 0.0 copy-done.1
  170.8 0.0 copy-start
  170.8 1.0 copy.22
  171.8 0.6 copy-done
  172.4 0.0 copy-start.2
  172.4 0.0 copy-start.3
  172.4 1.0 copy.23
  173.4 0.1 copy-done.2
  173.5 0.7 copy.24
  174.2 0.0 copy-done.3
  174.2 0.6 copy.25
Async XLA Ops:
  168.4 2.4 %copy-start.1 = (f32[512,512]{1,0:T(8,128)S(1)}, f32[512,512]{1,0:T(8,128)}, u32[]{:S(2)}) copy-start(f32[512,512]{1,0:T(8,128)} %get-tuple-element.51) | copy-start | bytes 3145732
  170.8 1.6 copy-start
  172.4 1.1 copy-start.2
  172.4 1.8 %copy-start.3 = (f32[16,1024]{1,0:T(8,128)S(1)}, f32[16,1024]{1,0:T(8,128)}, u32[]{:S(2)}) copy-start(f32[16,1024]{1,0:T(8,128)} %get-tuple-element.54) | copy-start | bytes 196612

commit v2 on v1

--- a/solution.py
+++ b/solution.py
@@ -11,6 +11,7 @@
 BF = jnp.bfloat16
 F32 = jnp.float32
 NEG = -1e30
+STATE = F32
 SEGS, HEADS, DK, FH, SEG, NM, PEERS = 32, 4, 128, 512, 512, 128, 4
 WIDE = HEADS * DK
 COLS = SEGS // HEADS
@@ -54,7 +55,9 @@
         er[h, DK:, :] = jnp.where(
             row == 0, first, jnp.where(row == 1, second, jnp.where(row == 2, third, 0.0))
         ).astype(BF)
-        bt[h * COLS : (h + 1) * COLS] = (tn(z[...], kh) * (1.0 / SEG)).reshape(COLS, PIECE, DK)
+        bt[h * COLS : (h + 1) * COLS] = (
+            (tn(z[...], kh) * (1.0 / SEG)).astype(BF).reshape(COLS, PIECE, DK)
+        )
 
 
 def remote(src, dst, send, recv, where):
@@ -79,8 +82,27 @@
     pl.semaphore_wait(barrier, SEGS - 1 + PEERS - 1)
 
 
-def retained(er_all, t):
-    return jnp.sum(er_all[t, DK:, :].astype(F32), axis=0, keepdims=True)
+def place(dev):
+    return lax.div(dev, 8), lax.rem(lax.div(dev, 2), 4), lax.rem(dev, 2)
+
+
+def slot(dev):
+    z, x, core = place(dev)
+    return x * COLS + z * 2 + core
+
+
+def er_slot(dev):
+    z, x, core = place(dev)
+    return core * 16 + z * 4 + x
+
+
+def step(old, er_all, t, add):
+    high = old.astype(BF)
+    low = (old - high.astype(F32)).astype(BF)
+    e = er_slot(t)
+    decay = nn(jnp.concatenate([high, low], axis=0), er_all[e, 0:DK, :])
+    share = jnp.sum(er_all[e, DK:, :].astype(F32), axis=0, keepdims=True)
+    return share * old - (decay[:PIECE] + decay[PIECE:]) + add.astype(F32)
 
 
 def sum_over_heads(block, mine, landing, gathered, my, s_y, r_y):
@@ -126,45 +148,88 @@
     er, bt, kk, vv, qq, gg, picked, readout,
     er_out, mt_out, k1, v1, k2, v2, q1, g1, q2, g2, hid, tok,
     er_all, bt_all, outb, mt, mine_y, land_y, gath_y, part, state,
-    s_er, r_er, s_bt, r_bt, s_m, r_m, s_halo, r_halo, s_y, r_y, loc,
+    s_er, r_er, s_bt, r_bt, s_m, r_m, s_halo, r_halo, s_y, r_y, s_z, r_z, loc,
 ):
     me, my = lax.axis_index("ctx"), lax.axis_index("head")
-    mine = lax.div(me, COLS)
-    core = lax.rem(me, 2)
+    mz, mx, core = place(me)
     partner = me + 1 - 2 * core
     enter(me, my)
 
-    def er_copy(to, src):
-        return remote(er.at[lax.div(to, COLS)], er_all.at[src], s_er.at[to], r_er.at[src], {"ctx": to})
+    def er_copy(x, to_x):
+        return remote(
+            er.at[to_x], er_all.at[core * 16 + mz * 4 + x], s_er.at[to_x], r_er.at[x],
+            {"ctx": mz * 8 + to_x * 2 + core},
+        )
+
+    def block(side, z):
+        return er_all.at[pl.ds(side * 16 + z * 4, 4)]
+
+    def over_z(d):
+        to = lax.rem(mz + d, 4)
+        return remote(
+            block(core, mz), block(core, mz), s_z.at[d], r_z.at[d], {"ctx": to * 8 + mx * 2 + core}
+        )
+
+    def over_core(d, side):
+        z = lax.rem(mz + 4 - d, 4)
+        return remote(block(side, z), block(side, z), s_z.at[4 + d], r_z.at[4 + d], {"ctx": partner})
 
     def bt_copy(to, src):
-        return remote(bt.at[to], bt_all.at[src], s_bt.at[to], r_bt.at[src], {"ctx": to})
+        return remote(bt.at[slot(to)], bt_all.at[src], s_bt.at[to], r_bt.at[src], {"ctx": to})
 
     def m_copy(to, src):
-        return remote(outb.at[to], mt.at[src], s_m.at[to], r_m.at[src], {"ctx": to})
+        return remote(outb.at[to], mt.at[slot(src)], s_m.at[to], r_m.at[src], {"ctx": to})
+
+    for d in range(1, 4):
+        er_copy(mx, lax.rem(mx + d, 4)).start()
+    own_er = pltpu.make_async_copy(er.at[mx], er_all.at[er_slot(me)], loc.at[0])
+    own_bt = pltpu.make_async_copy(bt.at[slot(me)], bt_all.at[me], loc.at[1])
+    own_er.start()
+    own_bt.start()
 
     @pl.loop(1, SEGS)
     def _(d):
-        to = lax.rem(me + d, SEGS)
-        er_copy(to, me).start()
-        bt_copy(to, me).start()
+        bt_copy(lax.rem(me + d, SEGS), me).start()
 
     def halo(src, dst, i, to):
         return remote(src, dst, s_halo.at[i], r_halo.at[i], {"ctx": to})
 
     after, before = lax.rem(me + 2, SEGS), lax.rem(me + SEGS - 2, SEGS)
     far = [
-        halo(kk, k2, 0, after),
-        halo(vv, v2, 1, after),
-        halo(qq, q2, 2, before),
-        halo(gg, g2, 3, before),
+        halo(vv, v2, 0, after),
+        halo(gg, g2, 1, before),
+        halo(kk, k2, 2, after),
+        halo(qq, q2, 3, before),
     ]
-    keys_near = [halo(kk, k1, 4, partner), halo(vv, v1, 5, partner)]
-    rows_near = [halo(qq, q1, 6, partner), halo(gg, g1, 7, partner)]
-    keys_relay = [halo(k2, k1, 4, partner), halo(v2, v1, 5, partner)]
-    rows_relay = [halo(q2, q1, 6, partner), halo(g2, g1, 7, partner)]
-    for copy in far:
+    keys_near = [halo(vv, v1, 4, partner), halo(kk, k1, 6, partner)]
+    rows_near = [halo(gg, g1, 5, partner), halo(qq, q1, 7, partner)]
+    keys_relay = [halo(v2, v1, 4, partner), halo(k2, k1, 6, partner)]
+    rows_relay = [halo(g2, g1, 5, partner), halo(q2, q1, 7, partner)]
+    for copy in far[:2]:
         copy.start()
+
+    def relay(i):
+        far[2 * i].wait_recv()
+        far[2 * i + 1].wait_recv()
+
+        @pl.when(core == 1)
+        def _():
+            keys_relay[i].start()
+
+        @pl.when(core == 0)
+        def _():
+            rows_relay[i].start()
+
+    own_er.wait()
+    own_bt.wait()
+    for d in range(1, 4):
+        er_copy(lax.rem(mx + 4 - d, 4), mx).wait_recv()
+    for d in range(1, 4):
+        over_z(d).start()
+    over_core(0, core).start()
+    for d in range(1, 4):
+        over_z(d).wait_recv()
+        over_core(d, core).start()
 
     @pl.when(core == 0)
     def _():
@@ -176,26 +241,21 @@
         for copy in rows_near:
             copy.start()
 
-    own_er = pltpu.make_async_copy(er.at[mine], er_all.at[me], loc.at[0])
-    own_bt = pltpu.make_async_copy(bt.at[me], bt_all.at[me], loc.at[1])
-    own_er.start()
-    own_bt.start()
-    own_er.wait()
-    own_bt.wait()
-
     @pl.loop(1, SEGS)
     def _(d):
         src = lax.rem(me + SEGS - d, SEGS)
-        er_copy(src, src).wait_recv()
         bt_copy(src, src).wait_recv()
+
+    for d in range(4):
+        over_core(d, 1 - core).wait_recv()
 
     state[...] = jnp.zeros((PIECE, DK), F32)
 
     @pl.loop(0, SEGS)
     def _(t):
         old = state[...]
-        outb[t] = old
-        state[...] = retained(er_all, t) * old - nn(old.astype(BF), er_all[t, 0:DK, :]) + bt_all[t]
+        outb[t] = old.astype(outb.dtype)
+        state[...] = step(old, er_all, t, bt_all[t])
 
         @pl.when((t > 0) & (t - 1 != me))
         def _():
@@ -205,14 +265,16 @@
     def _():
         m_copy(SEGS - 1, me).start()
 
-    own_m = pltpu.make_async_copy(outb.at[me], mt.at[me], loc.at[2])
+    own_m = pltpu.make_async_copy(outb.at[me], mt.at[slot(me)], loc.at[2])
     own_m.start()
+    for copy in far[2:]:
+        copy.start()
+    er_out[...] = er_all[...]
     own_m.wait()
 
     @pl.loop(1, SEGS)
     def _(d):
         to = lax.rem(me + d, SEGS)
-        er_copy(to, me).wait_send()
         bt_copy(to, me).wait_send()
         m_copy(to, me).wait_send()
         m_copy(to, to).wait_recv()
@@ -220,9 +282,10 @@
     for h in range(HEADS):
         m_h = mt[h * COLS : (h + 1) * COLS].reshape(FH, DK)
         high = m_h.astype(BF)
-        low = (m_h - high.astype(F32)).astype(BF)
         mt_out[h * COLS : (h + 1) * COLS] = high.reshape(COLS, PIECE, DK)
-        term = nt(picked[:, head(h)], high) + nt(picked[:, head(h)], low)
+        term = nt(picked[:, head(h)], high)
+        if STATE == F32:
+            term += nt(picked[:, head(h)], (m_h - high.astype(F32)).astype(BF))
         for j in range(PEERS):
             if h == 0:
                 part[j] = term[:, head(j)]
@@ -230,25 +293,17 @@
                 part[j] += term[:, head(j)]
     started, summed, finished = sum_over_heads(lambda j: part[j], mine_y, land_y, gath_y, my, s_y, r_y)
     started()
-    er_out[...] = er_all[...]
+    relay(0)
     summed()
-
-    for copy in far:
-        copy.wait_recv()
-
-    @pl.when(core == 1)
-    def _():
-        for copy in keys_relay:
-            copy.start()
-
-    @pl.when(core == 0)
-    def _():
-        for copy in rows_relay:
-            copy.start()
-
     low = finished()
     hid[...] = low
     tok[...] = nn(low, readout[...]).astype(BF)
+    relay(1)
+    for d in range(1, 4):
+        er_copy(mx, lax.rem(mx + d, 4)).wait_send()
+        over_z(d).wait_send()
+    for d in range(4):
+        over_core(d, core).wait_send()
     for copy in far:
         copy.wait_send()
     for copy in keys_near + rows_near:
@@ -259,7 +314,7 @@
     scale = DK**-0.5
     segment = lax.axis_index("ctx")
     uses = [
-        (allowed[segment, offset] == 1) & (segment > offset) for offset in range(2)
+        (allowed[0, offset] == 1) & (segment > offset) for offset in range(2)
     ]
     q_t, g_t = q[...], g[...]
     causal = lax.broadcasted_iota(jnp.int32, (SEG, SEG), 0) >= lax.broadcasted_iota(
@@ -302,7 +357,7 @@
     dq_h, dk_h, dv_h,
     out_q, out_k, out_v, out_z, out_r,
     er_all, mt, kk, vv, zz, q1, g1, q2, g2, dq, dk, dv,
-    part, mine_y, land_y, gath_y, gsb, gs_all, gout, gt, rbuf, rall, tparts, st_in, state,
+    part, mine_y, land_y, gath_y, gsb, gs_all, gout, gt, rterm, rlow, rpair, rbuf, rall, tparts, st_in, state,
     s_gs, r_gs, s_g, r_g, s_r, r_r, s_y, r_y, s_t, r_t, s_st, r_st, loc, fetch,
 ):
     me, my = lax.axis_index("ctx"), lax.axis_index("head")
@@ -325,13 +380,18 @@
         return remote(stats, st_in.at[o - 1], s_st.at[o - 1], r_st.at[o - 1], {"ctx": to})
 
     def gs_copy(to, src):
-        return remote(gsb.at[to], gs_all.at[src], s_gs.at[to], r_gs.at[src], {"ctx": to})
+        return remote(gsb.at[slot(to)], gs_all.at[src], s_gs.at[to], r_gs.at[src], {"ctx": to})
 
     def g_copy(to, src):
-        return remote(gout.at[to], gt.at[src], s_g.at[to], r_g.at[src], {"ctx": to})
-
-    def r_copy(to, src):
-        return remote(rbuf.at[to], rall.at[src], s_r.at[to], r_r.at[src], {"ctx": to})
+        return remote(gout.at[to], gt.at[slot(src)], s_g.at[to], r_g.at[src], {"ctx": to})
+
+    core = lax.rem(me, 2)
+    chip = lax.div(me, 2)
+    pair = remote(rlow.at[1 - core], rpair, s_r.at[0], r_r.at[0], {"ctx": me + 1 - 2 * core})
+
+    def r_copy(d):
+        to = lax.rem(chip + d, SEGS // 2)
+        return remote(rbuf.at[to], rall.at[chip], s_r.at[d], r_r.at[d], {"ctx": to * 2 + core})
 
     def far_tile(o, h):
         q_t, g_t = (q1, g1) if o == 1 else (q2, g2)
@@ -350,7 +410,11 @@
     started()
     for o in (1, 2):
         stat_copy(o).start()
-    rbuf[...] = tn(hid[...], gm[...]).astype(BF).reshape(SEGS, FH // SEGS, 2 * WIDE)
+    term = tn(hid[...], gm[...]).reshape(SEGS // 2, 2, FH // SEGS, 2 * WIDE)
+    for side in range(2):
+        rterm[side] = term[:, side]
+        rlow[side] = term[:, side].astype(BF)
+    pair.start()
     for copy in fetched[:8]:
         copy.wait()
     for o in (1, 2):
@@ -369,12 +433,15 @@
     def _(d):
         gs_copy(lax.rem(me + d, SEGS), me).start()
 
-    @pl.loop(1, SEGS)
-    def _(d):
-        r_copy(lax.rem(me + d, SEGS), me).start()
-
-    own_gs = pltpu.make_async_copy(gsb.at[me], gs_all.at[me], loc.at[0])
-    own_r = pltpu.make_async_copy(rbuf.at[me], rall.at[me], loc.at[1])
+    own_gs = pltpu.make_async_copy(gsb.at[slot(me)], gs_all.at[me], loc.at[0])
+    pair.wait()
+    rbuf[...] = (rterm[core] + rpair[...].astype(F32)).astype(BF)
+
+    @pl.loop(1, SEGS // 2)
+    def _(d):
+        r_copy(d).start()
+
+    own_r = pltpu.make_async_copy(rbuf.at[chip], rall.at[chip], loc.at[1])
     own_gs.start()
     own_r.start()
 
@@ -398,9 +465,8 @@
     def _(i):
         t = SEGS - 1 - i
         old = state[...]
-        low = old.astype(BF)
-        gout[t] = low
-        state[...] = retained(er_all, t) * old - nn(low, er_all[t, 0:DK, :]) + gs_all[t].astype(F32)
+        gout[t] = old.astype(BF)
+        state[...] = step(old, er_all, t, gs_all[t])
 
         @pl.when((i > 0) & (t + 1 != me))
         def _():
@@ -410,7 +476,7 @@
     def _():
         g_copy(0, me).start()
 
-    own_g = pltpu.make_async_copy(gout.at[me], gt.at[me], loc.at[2])
+    own_g = pltpu.make_async_copy(gout.at[me], gt.at[slot(me)], loc.at[2])
     own_g.start()
 
     onehot = (
@@ -456,11 +522,9 @@
             - nn(kk[:, head(h)], both) * (rate[0, h] / SEG)
         )
 
-    @pl.loop(1, SEGS)
-    def _(d):
-        to = lax.rem(me + d, SEGS)
-        r_copy(to, me).wait_send()
-        r_copy(to, to).wait_recv()
+    @pl.loop(1, SEGS // 2)
+    def _(d):
+        r_copy(d).wait()
 
     out_r[...] = jnp.sum(rall[...].astype(F32), axis=0)
 
@@ -470,6 +534,12 @@
     for d in range(1, PEERS):
         grad += tparts[PEERS + d].astype(F32)
     out_z[...] = grad
+
+
+def finish_kernel(*refs):
+    half = len(refs) // 2
+    for src, dst in zip(refs[:half], refs[half:]):
+        dst[...] = src[...]
 
 
 def shape(dims, kind):
@@ -488,7 +558,7 @@
         prep_kernel,
         out_shape=(
             shape((HEADS, DK + ROWS_R, DK), BF),
-            shape((SEGS, PIECE, DK), F32),
+            shape((SEGS, PIECE, DK), BF),
             shape((NM, WIDE), BF),
         ),
         in_specs=[SM, SM, VM, VM, VM, VM],
@@ -516,16 +586,16 @@
         out_specs=(VM, VM) + (ANY,) * 8 + (VM, VM),
         scratch_shapes=[
             pltpu.VMEM((SEGS, DK + ROWS_R, DK), BF),
-            pltpu.VMEM((SEGS, PIECE, DK), F32),
-            pltpu.VMEM((SEGS, PIECE, DK), F32),
-            pltpu.VMEM((SEGS, PIECE, DK), F32),
+            pltpu.VMEM((SEGS, PIECE, DK), BF),
+            pltpu.VMEM((SEGS, PIECE, DK), STATE),
+            pltpu.VMEM((SEGS, PIECE, DK), STATE),
         ]
         + sums
         + [
             pltpu.VMEM((PEERS, NM, FH // PEERS), F32),
             pltpu.VMEM((PIECE, DK), F32),
-            dma(SEGS), dma(SEGS), dma(SEGS), dma(SEGS), dma(SEGS), dma(SEGS),
-            dma(8), dma(8), dma(2 * PEERS), dma(2 * PEERS), dma(3),
+            dma(4), dma(4), dma(SEGS), dma(SEGS), dma(SEGS), dma(SEGS),
+            dma(8), dma(8), dma(2 * PEERS), dma(2 * PEERS), dma(8), dma(8), dma(3),
         ],
         compiler_params=pltpu.CompilerParams(
             collective_id=0, has_side_effects=True, vmem_limit_bytes=LIMIT
@@ -533,6 +603,7 @@
         name="forward_scan",
     )(er, bt, key_rows, value_rows, queries, grad_out, picked, readout)
 
+    own_allowed = lax.dynamic_slice(allowed, (lax.axis_index("ctx"), 0), (1, 2))
     one = pl.BlockSpec((SEG, DK), lambda h: (0, h))
     wide = pl.BlockSpec((NM, 2 * DK), lambda h: (0, h))
     dq, dk, dv, gm, stats = pl.pallas_call(
@@ -549,17 +620,18 @@
         out_specs=(one,) * 3 + (wide, pl.BlockSpec((8, SEG), lambda h: (h, 0))),
         compiler_params=pltpu.CompilerParams(vmem_limit_bytes=LIMIT),
         name="attention",
-    )(allowed, queries, grad_out, key_rows, value_rows, k1, v1, k2, v2, tok)
-
-    return pl.pallas_call(
+    )(own_allowed, queries, grad_out, key_rows, value_rows, k1, v1, k2, v2, tok)
+
+    results = (
+        shape(block, F32),
+        shape(block, F32),
+        shape(block, F32),
+        shape((SEG, FH // PEERS), F32),
+        shape((FH // SEGS, 2 * WIDE), F32),
+    )
+    outs = pl.pallas_call(
         backward_kernel,
-        out_shape=(
-            shape(block, F32),
-            shape(block, F32),
-            shape(block, F32),
-            shape((SEG, FH // PEERS), F32),
-            shape((FH // SEGS, 2 * WIDE), F32),
-        ),
+        out_shape=results,
         in_specs=[SM] + [VM] * 6 + [ANY] * 12,
         out_specs=(VM,) * 5,
         scratch_shapes=[
@@ -575,12 +647,15 @@
             pltpu.VMEM((SEGS, PIECE, DK), BF),
             pltpu.VMEM((SEGS, PIECE, DK), BF),
             pltpu.VMEM((SEGS, PIECE, DK), BF),
-            pltpu.VMEM((SEGS, FH // SEGS, 2 * WIDE), BF),
-            pltpu.VMEM((SEGS, FH // SEGS, 2 * WIDE), BF),
+            pltpu.VMEM((2, SEGS // 2, FH // SEGS, 2 * WIDE), F32),
+            pltpu.VMEM((2, SEGS // 2, FH // SEGS, 2 * WIDE), BF),
+            pltpu.VMEM((SEGS // 2, FH // SEGS, 2 * WIDE), BF),
+            pltpu.VMEM((SEGS // 2, FH // SEGS, 2 * WIDE), BF),
+            pltpu.VMEM((SEGS // 2, FH // SEGS, 2 * WIDE), BF),
             pltpu.VMEM((2 * PEERS, SEG, FH // PEERS), BF),
             pltpu.VMEM((2, 8 * HEADS, SEG), F32),
             pltpu.VMEM((PIECE, DK), F32),
-            dma(SEGS), dma(SEGS), dma(SEGS), dma(SEGS), dma(SEGS), dma(SEGS),
+            dma(SEGS), dma(SEGS), dma(SEGS), dma(SEGS), dma(SEGS // 2), dma(SEGS // 2),
             dma(2 * PEERS), dma(2 * PEERS), dma(PEERS), dma(PEERS), dma(2), dma(2), dma(3), dma(12),
         ],
         compiler_params=pltpu.CompilerParams(
@@ -591,6 +666,14 @@
         learn_rate, gm, readout, picked, hid, positions, stats, er_all, mt, key_rows, value_rows, targets,
         q1, g1, q2, g2, dq, dk, dv,
     )
+    specs = (
+        (one,) * 3
+        + (pl.BlockSpec((SEG // HEADS, FH // PEERS), lambda h: (h, 0)),)
+        + (pl.BlockSpec((FH // SEGS, 2 * DK), lambda h: (0, h)),)
+    )
+    return pl.pallas_call(
+        finish_kernel, grid=(HEADS,), out_shape=results, in_specs=list(specs), out_specs=specs, name="finish"
+    )(*outs)
 
 
 def solution(mesh):

time: 175 us -> 157 us (0.90)
  Pallas kernels: 166 us -> 154 us
  local copies, waits for them, and re-layouts: 7.74 us -> 1.37 us
    pallas_call x1, Pallas kernels: 88.2 us -> 70.7 us  [on_device(): pl.pallas_call(forward_kernel, out_shape=(shape((SEGS, DK + ROWS_R, DK),...]
    unnamed x14 -> x3, local copies, waits for them, and re-layouts: 7.74 us -> 1.3 us
    pallas_call x1 -> x2, Pallas kernels: 59.4 us -> 65 us  [the longest x1 60.7 us: on_device(): pl.pallas_call(backward_kernel, out_shape=results, in_specs=[SM] + [VM] *...]
where the time goes in v2:
time: 157 us; the launch traced here: 156 us
  Pallas kernels  154 us (98%)
    pallas_call x1, Pallas kernels, on_device(): pl.pallas_call(forward_kernel, out_shape=(shape((SEGS, DK + ROWS_R, DK),...  70.7 us
    pallas_call x1, Pallas kernels, on_device(): pl.pallas_call(backward_kernel, out_shape=results, in_specs=[SM] + [VM] *...  60.7 us
    pallas_call x1, Pallas kernels, on_device(): pl.pallas_call(attention_kernel, grid=(HEADS,), out_shape=(shape(block, F...  15.4 us
    pallas_call x1, Pallas kernels, on_device(): pl.pallas_call(finish_kernel, grid=(HEADS,), out_shape=results, in_specs=...  4.3 us
    pallas_call x1, Pallas kernels, on_device(): pl.pallas_call(prep_kernel, out_shape=(shape((HEADS, DK + ROWS_R, DK), BF...  3.17 us

profile of v2, /device:TPU:0, one launch (start us, length us, event | category | flops | bytes accessed | tf_op | source)
XLA Modules:
  0.0 156.5 jit_solution(17834942711977506081)
XLA Ops:
  0.6 0.0 copy-start
  0.7 0.7 copy-done
  1.3 0.1 constant_dynamic-slice_fusion
  1.4 0.6 copy.16.allowed
  2.0 3.2 %prep.1 = (bf16[4,144,128]{2,1,0:T(8,128)(2,1)}, bf16[32,64,128]{2,1,0:T(8,128)(2,1)}, bf16[128,512]{1,0:T(8,128)(2,1)}) custom-call(f32[1,4]{1,0:T(1,128)} %retain.1, f32[1,4]{1,0:T(1,128)} %rate.3, bf16[512,512]{1,0:T(8,128)(2,1)} %q.3, bf16[512,512]{1,0:T(8,128)(2,1)} %kk_h.1, bf16[512,512]{1,0:T(8,128)(2,1)} %zz_h.1, s32[1,128]{1,0:T(1,128)} %pos.3), custom_call_target="tpu_custom_call" | custom-call | tf_op jit(solution)/shard_map/prep/pallas_call | solution.py:557
  5.2 70.7 %forward_scan.1 = (bf16[32,144,128]{2,1,0:T(8,128)(2,1)}, bf16[32,64,128]{2,1,0:T(8,128)(2,1)}, bf16[512,512]{1,0:T(8,128)(2,1)}, bf16[512,512]{1,0:T(8,128)(2,1...) custom-call(bf16[4,144,128]{2,1,0:T(8,128)(2,1)} %get-tuple-element., ...), custom_call_target="tpu_custom_call" | custom-call | tf_op jit(solution)/shard_map/forward_scan/pallas_call | solution.py:574
  75.9 15.4 %attention.1 = (f32[512,512]{1,0:T(8,128)}, f32[512,512]{1,0:T(8,128)}, f32[512,512]{1,0:T(8,128)}, bf16[128,1024]{1,0:T(8,128)(2,1)}, f32[32,512]{1,0:T(8,128)}) custom-call(s32[1,2]{1,0:T(1,128)} %copy.16.allowed, bf16[512,512]{1,0:T(8,128)(2,1)} %q.3, bf16[512,512]{1,0:T(8,128)(2,1)} %g.1, bf16[512,512]{1,0:T(8,128)(2,1)} %kk_h.1, bf16[512,512]{1,0:T(8,128)(2,1)} %vv_h.1, ...), custom_call_target="tpu_custom_call" | custom-call | tf_op jit(solution)/shard_map/attention/pallas_call | solution.py:609
  91.3 60.7 %backward_scan.1 = (f32[512,512]{1,0:T(8,128)}, f32[512,512]{1,0:T(8,128)}, f32[512,512]{1,0:T(8,128)}, f32[512,128]{1,0:T(8,128)}, f32[16,1024]{1,0:T(8,128)}) custom-call(f32[1,4]{1,0:T(1,128)} %rate.3, bf16[128,1024]{1,0:T(8,128)(2,1)} %get-tuple-element.38.gm, bf16[512,1024]{1,0:T(8,128)(2,1)} %readout.3, bf16[128,512]{1,0:T(8,128)(2,1)} %get-tuple-element.32.picked, ...), custom_call_target="tpu_custom_call" | custom-call | tf_op jit(solution)/shard_map/backward_scan/pallas_call | solution.py:632
  152.1 4.3 %finish.1 = (f32[512,512]{1,0:T(8,128)}, f32[512,512]{1,0:T(8,128)}, f32[512,512]{1,0:T(8,128)}, f32[512,128]{1,0:T(8,128)}, f32[16,1024]{1,0:T(8,128)}) custom-call(f32[512,512]{1,0:T(8,128)} %get-tuple-element.50.refs_0_, f32[512,512]{1,0:T(8,128)} %get-tuple-element.51.refs_1_, f32[512,512]{1,0:T(8,128)} %get-tuple-element.52.refs_2_, ...), custom_call_target="tpu_custom_call" | custom-call | tf_op jit(solution)/shard_map/finish/pallas_call | solution.py:674
Async XLA Ops:
  0.6 0.7 copy-start

commit v3 on v2

--- a/solution.py
+++ b/solution.py
@@ -39,11 +39,10 @@
     return slice(h * DK, (h + 1) * DK)
 
 
-def prep_kernel(retain, rate, q, k, z, pos, er, bt, picked):
+def local_maps(retain, rate, q, k, z, pos, er, bt, picked):
     onehot = (
         lax.broadcasted_iota(jnp.int32, (SEG, NM), 0) == pos[...]
     ).astype(F32).astype(BF)
-    picked[...] = tn(onehot, q[...]).astype(BF)
     row = lax.broadcasted_iota(jnp.int32, (ROWS_R, DK), 0)
     for h in range(HEADS):
         kh = k[:, head(h)]
@@ -55,9 +54,11 @@
         er[h, DK:, :] = jnp.where(
             row == 0, first, jnp.where(row == 1, second, jnp.where(row == 2, third, 0.0))
         ).astype(BF)
+    for h in range(HEADS):
         bt[h * COLS : (h + 1) * COLS] = (
-            (tn(z[...], kh) * (1.0 / SEG)).astype(BF).reshape(COLS, PIECE, DK)
-        )
+            (tn(z[...], k[:, head(h)]) * (1.0 / SEG)).astype(BF).reshape(COLS, PIECE, DK)
+        )
+    picked[...] = tn(onehot, q[...]).astype(BF)
 
 
 def remote(src, dst, send, recv, where):
@@ -66,7 +67,7 @@
     )
 
 
-def enter(me, my):
+def greet(me, my):
     barrier = pltpu.get_barrier_semaphore()
 
     @pl.loop(1, SEGS)
@@ -79,7 +80,7 @@
         pl.semaphore_signal(
             barrier, inc=1, device_id={"head": lax.rem(my + d, PEERS)}, device_id_type=MESH
         )
-    pl.semaphore_wait(barrier, SEGS - 1 + PEERS - 1)
+    return lambda: pl.semaphore_wait(barrier, SEGS - 1 + PEERS - 1)
 
 
 def place(dev):
@@ -145,15 +146,17 @@
 
 
 def forward_kernel(
-    er, bt, kk, vv, qq, gg, picked, readout,
-    er_out, mt_out, k1, v1, k2, v2, q1, g1, q2, g2, hid, tok,
-    er_all, bt_all, outb, mt, mine_y, land_y, gath_y, part, state,
+    retain, rate, q, k, z, pos, kk, vv, qq, gg, readout,
+    er_out, mt_out, k1, v1, k2, v2, q1, g1, q2, g2, hid, tok, picked,
+    er, bt, er_all, bt_all, outb, mt, mine_y, land_y, gath_y, part, state,
     s_er, r_er, s_bt, r_bt, s_m, r_m, s_halo, r_halo, s_y, r_y, s_z, r_z, loc,
 ):
     me, my = lax.axis_index("ctx"), lax.axis_index("head")
     mz, mx, core = place(me)
     partner = me + 1 - 2 * core
-    enter(me, my)
+    entered = greet(me, my)
+    local_maps(retain, rate, q, k, z, pos, er, bt, picked)
+    entered()
 
     def er_copy(x, to_x):
         return remote(
@@ -267,8 +270,6 @@
 
     own_m = pltpu.make_async_copy(outb.at[me], mt.at[slot(me)], loc.at[2])
     own_m.start()
-    for copy in far[2:]:
-        copy.start()
     er_out[...] = er_all[...]
     own_m.wait()
 
@@ -279,6 +280,8 @@
         m_copy(to, me).wait_send()
         m_copy(to, to).wait_recv()
 
+    for copy in far[2:]:
+        copy.start()
     for h in range(HEADS):
         m_h = mt[h * COLS : (h + 1) * COLS].reshape(FH, DK)
         high = m_h.astype(BF)
@@ -310,70 +313,72 @@
         copy.wait()
 
 
-def attention_kernel(allowed, q, g, k, v, k1, v1, k2, v2, tok, dq, dk, dv, gm, stats):
-    scale = DK**-0.5
-    segment = lax.axis_index("ctx")
-    uses = [
-        (allowed[0, offset] == 1) & (segment > offset) for offset in range(2)
-    ]
-    q_t, g_t = q[...], g[...]
-    causal = lax.broadcasted_iota(jnp.int32, (SEG, SEG), 0) >= lax.broadcasted_iota(
-        jnp.int32, (SEG, SEG), 1
-    )
-    keys = [tok[:, 0:DK], k[...], k1[...], k2[...]]
-    vals = [tok[:, DK:], v[...], v1[...], v2[...]]
-    scores = [nt(q_t, key) for key in keys]
-    scores[1] = jnp.where(causal, scores[1], NEG)
-    scores[2] = jnp.where(uses[0], scores[2], NEG)
-    scores[3] = jnp.where(uses[1], scores[3], NEG)
-    top = functools.reduce(jnp.maximum, [jnp.max(s, axis=1, keepdims=True) for s in scores])
-    exps = [jnp.exp((s - top) * scale) for s in scores]
-    total = functools.reduce(jnp.add, [jnp.sum(e, axis=1, keepdims=True) for e in exps])
-    inverse = 1.0 / total
-    probs = [e * inverse for e in exps]
-    lows = [p.astype(BF) for p in probs]
-    attended = functools.reduce(jnp.add, [nn(p, value) for p, value in zip(lows, vals)])
-    delta = jnp.sum(g_t.astype(F32) * attended, axis=1, keepdims=True)
-    grads = [
-        (p * (nt(g_t, value) - delta)).astype(BF) for p, value in zip(probs, vals)
-    ]
-    gm[:, 0:DK] = (tn(grads[0], q_t) * scale).astype(BF)
-    gm[:, DK:] = tn(lows[0], g_t).astype(BF)
-    dq[...] = functools.reduce(jnp.add, [nn(s, key) for s, key in zip(grads, keys)]) * scale
-    dk[...] = tn(grads[1], q_t) * scale
-    dv[...] = tn(lows[1], g_t)
-    level = top * scale + jnp.log(total)
-    lane = lax.broadcasted_iota(jnp.int32, (SEG, DK), 1)
-    columns = jnp.where(
-        lane == 0,
-        jnp.where(uses[0], level, -NEG),
-        jnp.where(lane == 1, jnp.where(uses[1], level, -NEG), delta),
-    )
-    stats[...] = columns.T[0:8, :]
-
-
 def backward_kernel(
-    rate, gm, readout, picked, hid, pos, stats, er_all_h, mt_h, kk_h, vv_h, zz_h, q1_h, g1_h, q2_h, g2_h,
-    dq_h, dk_h, dv_h,
+    rate, bias, tok, readout, picked, hid, pos,
+    q_h, g_h, k_h, v_h, k1_h, v1_h, k2_h, v2_h, q1_h, g1_h, q2_h, g2_h, mt_h, er_all_h, zz_h,
     out_q, out_k, out_v, out_z, out_r,
-    er_all, mt, kk, vv, zz, q1, g1, q2, g2, dq, dk, dv,
+    qq, gg, kk, vv, k1, v1, k2, v2, q1, g1, q2, g2, mt, er_all, zz,
+    gm, stats, scores_grad, own_probs,
     part, mine_y, land_y, gath_y, gsb, gs_all, gout, gt, rterm, rlow, rpair, rbuf, rall, tparts, st_in, state,
     s_gs, r_gs, s_g, r_g, s_r, r_r, s_y, r_y, s_t, r_t, s_st, r_st, loc, fetch,
 ):
     me, my = lax.axis_index("ctx"), lax.axis_index("head")
     scale = DK**-0.5
+    entered = greet(me, my)
     fetched = [
         pltpu.make_async_copy(src, dst, fetch.at[i])
         for i, (src, dst) in enumerate(
             (
-                (kk_h, kk), (vv_h, vv), (q1_h, q1), (g1_h, g1), (q2_h, q2), (g2_h, g2), (dk_h, dk), (dv_h, dv),
-                (mt_h, mt), (dq_h, dq), (er_all_h, er_all), (zz_h, zz),
+                (q_h, qq), (k_h, kk), (k1_h, k1), (k2_h, k2), (v_h, vv), (v1_h, v1), (v2_h, v2), (g_h, gg),
+                (q1_h, q1), (g1_h, g1), (q2_h, q2), (g2_h, g2), (mt_h, mt), (er_all_h, er_all), (zz_h, zz),
             )
         )
     ]
     for copy in fetched:
         copy.start()
-    enter(me, my)
+    for copy in fetched[:8]:
+        copy.wait()
+
+    @pl.loop(0, HEADS)
+    def _(h):
+        lanes = pl.ds(pl.multiple_of(h * DK, DK), DK)
+        tok_k = pl.ds(pl.multiple_of(h * 2 * DK, DK), DK)
+        tok_v = pl.ds(pl.multiple_of(h * 2 * DK + DK, DK), DK)
+        q_t, g_t = qq[:, lanes], gg[:, lanes]
+        causal = lax.broadcasted_iota(jnp.int32, (SEG, SEG), 0) >= lax.broadcasted_iota(
+            jnp.int32, (SEG, SEG), 1
+        )
+        keys = [kk[:, lanes], k1[:, lanes], k2[:, lanes], tok[:, tok_k]]
+        vals = [vv[:, lanes], v1[:, lanes], v2[:, lanes], tok[:, tok_v]]
+        scores = [nt(q_t, key) for key in keys]
+        scores[0] = jnp.where(causal, scores[0], NEG)
+        scores[1] = scores[1] + bias[0, 0]
+        scores[2] = scores[2] + bias[0, 1]
+        top = functools.reduce(jnp.maximum, [jnp.max(s, axis=1, keepdims=True) for s in scores])
+        exps = [jnp.exp((s - top) * scale) for s in scores]
+        total = functools.reduce(jnp.add, [jnp.sum(e, axis=1, keepdims=True) for e in exps])
+        inverse = 1.0 / total
+        probs = [e * inverse for e in exps]
+        lows = [p.astype(BF) for p in probs]
+        attended = functools.reduce(jnp.add, [nn(p, value) for p, value in zip(lows, vals)])
+        delta = jnp.sum(g_t.astype(F32) * attended, axis=1, keepdims=True)
+        grads = [
+            (p * (nt(g_t, value) - delta)).astype(BF) for p, value in zip(probs, vals)
+        ]
+        gm[:, tok_k] = (tn(grads[3], q_t) * scale).astype(BF)
+        gm[:, tok_v] = tn(lows[3], g_t).astype(BF)
+        own_probs[h] = lows[0]
+        for i in range(3):
+            scores_grad[h, :, i * SEG : (i + 1) * SEG] = grads[i]
+        scores_grad[h, :, 3 * SEG :] = grads[3]
+        level = top * scale + jnp.log(total)
+        lane = lax.broadcasted_iota(jnp.int32, (SEG, DK), 1)
+        columns = jnp.where(
+            lane == 0, level - bias[0, 0], jnp.where(lane == 1, level - bias[0, 1], delta)
+        )
+        stats[pl.ds(pl.multiple_of(h * 8, 8), 8), :] = columns.T[0:8, :]
+
+    entered()
 
     def stat_copy(o):
         to = lax.rem(me + SEGS - o, SEGS)
@@ -392,6 +397,17 @@
     def r_copy(d):
         to = lax.rem(chip + d, SEGS // 2)
         return remote(rbuf.at[to], rall.at[chip], s_r.at[d], r_r.at[d], {"ctx": to * 2 + core})
+
+    def own_tile(h):
+        grad = scores_grad[h, :, 0:SEG]
+        out_q[:, head(h)] = (
+            nn(grad, kk[:, head(h)])
+            + nn(scores_grad[h, :, SEG : 2 * SEG], k1[:, head(h)])
+            + nn(scores_grad[h, :, 2 * SEG : 3 * SEG], k2[:, head(h)])
+            + nn(scores_grad[h, :, 3 * SEG :], tok[:, 2 * h * DK : (2 * h + 1) * DK])
+        ) * scale
+        out_k[:, head(h)] = tn(grad, qq[:, head(h)]) * scale
+        out_v[:, head(h)] = tn(own_probs[h], gg[:, head(h)])
 
     def far_tile(o, h):
         q_t, g_t = (q1, g1) if o == 1 else (q2, g2)
@@ -400,8 +416,8 @@
         delta = st_in[o - 1, 8 * h + 2 : 8 * h + 3, :]
         probs = jnp.exp(nt(kk[:, head(h)], q_t) * scale - level)
         grads = probs * (nt(vv[:, head(h)], g_t) - delta)
-        dv[:, head(h)] += nn(probs.astype(BF), g_t)
-        dk[:, head(h)] += nn(grads.astype(BF), q_t) * scale
+        out_v[:, head(h)] += nn(probs.astype(BF), g_t)
+        out_k[:, head(h)] += nn(grads.astype(BF), q_t) * scale
 
     term = nt(gm[...], readout[...])
     for j in range(PEERS):
@@ -415,13 +431,11 @@
         rterm[side] = term[:, side]
         rlow[side] = term[:, side].astype(BF)
     pair.start()
-    for copy in fetched[:8]:
-        copy.wait()
-    for o in (1, 2):
-        stat_copy(o).wait()
+    own_tile(0)
+    own_tile(1)
     summed()
-    far_tile(1, 0)
-    far_tile(2, 0)
+    own_tile(2)
+    own_tile(3)
     gh = finished()
 
     for h in range(HEADS):
@@ -434,22 +448,26 @@
         gs_copy(lax.rem(me + d, SEGS), me).start()
 
     own_gs = pltpu.make_async_copy(gsb.at[slot(me)], gs_all.at[me], loc.at[0])
+    own_gs.start()
+    for o in (1, 2):
+        stat_copy(o).wait()
+    for copy in fetched[8:]:
+        copy.wait()
+    far_tile(1, 0)
+    far_tile(2, 0)
     pair.wait()
     rbuf[...] = (rterm[core] + rpair[...].astype(F32)).astype(BF)
+    far_tile(1, 1)
 
     @pl.loop(1, SEGS // 2)
     def _(d):
         r_copy(d).start()
 
     own_r = pltpu.make_async_copy(rbuf.at[chip], rall.at[chip], loc.at[1])
-    own_gs.start()
     own_r.start()
-
-    for h in range(1, HEADS):
-        far_tile(1, h)
-        far_tile(2, h)
-    for copy in fetched[8:]:
-        copy.wait()
+    far_tile(2, 1)
+    far_tile(1, 2)
+    far_tile(2, 2)
 
     own_gs.wait()
     own_r.wait()
@@ -478,6 +496,8 @@
 
     own_g = pltpu.make_async_copy(gout.at[me], gt.at[slot(me)], loc.at[2])
     own_g.start()
+    far_tile(1, 3)
+    far_tile(2, 3)
 
     onehot = (
         lax.broadcasted_iota(jnp.int32, (SEG, NM), 0) == pos[...]
@@ -485,8 +505,7 @@
     for h in range(HEADS):
         m_h = mt[h * COLS : (h + 1) * COLS].reshape(FH, DK)
         grad_picked = nn(gh, m_h).astype(BF)
-        out_q[:, head(h)] = dq[:, head(h)] + nn(onehot, grad_picked)
-    out_v[...] = dv[...]
+        out_q[:, head(h)] += nn(onehot, grad_picked)
 
     own_g.wait()
 
@@ -516,10 +535,8 @@
         g_h = gt[h * COLS : (h + 1) * COLS].reshape(FH, DK)
         m_h = mt[h * COLS : (h + 1) * COLS].reshape(FH, DK)
         both = (tn(g_h, m_h) + tn(m_h, g_h)).astype(BF)
-        out_k[:, head(h)] = (
-            dk[:, head(h)]
-            + nn(zz[...], g_h) * (1.0 / SEG)
-            - nn(kk[:, head(h)], both) * (rate[0, h] / SEG)
+        out_k[:, head(h)] += nn(zz[...], g_h) * (1.0 / SEG) - nn(kk[:, head(h)], both) * (
+            rate[0, h] / SEG
         )
 
     @pl.loop(1, SEGS // 2)
@@ -554,24 +571,12 @@
     queries, key_rows, value_rows, targets, readout, retain, learn_rate, allowed, positions, grad_out
 ):
     block = (SEG, WIDE)
-    er, bt, picked = pl.pallas_call(
-        prep_kernel,
-        out_shape=(
-            shape((HEADS, DK + ROWS_R, DK), BF),
-            shape((SEGS, PIECE, DK), BF),
-            shape((NM, WIDE), BF),
-        ),
-        in_specs=[SM, SM, VM, VM, VM, VM],
-        out_specs=(VM, VM, VM),
-        name="prep",
-    )(retain, learn_rate, queries, key_rows, targets, positions)
-
     sums = [
         pltpu.VMEM((PEERS, NM, FH // PEERS), F32),
         pltpu.VMEM((PEERS, NM, FH // PEERS), F32),
         pltpu.VMEM((PEERS, NM, FH // PEERS), BF),
     ]
-    er_all, mt, k1, v1, k2, v2, q1, g1, q2, g2, hid, tok = pl.pallas_call(
+    er_all, mt, k1, v1, k2, v2, q1, g1, q2, g2, hid, tok, picked = pl.pallas_call(
         forward_kernel,
         out_shape=(
             shape((SEGS, DK + ROWS_R, DK), BF),
@@ -581,10 +586,13 @@
         + (
             shape((NM, FH), BF),
             shape((NM, 2 * WIDE), BF),
+            shape((NM, WIDE), BF),
         ),
-        in_specs=[VM, VM, ANY, ANY, ANY, ANY, VM, VM],
-        out_specs=(VM, VM) + (ANY,) * 8 + (VM, VM),
+        in_specs=[SM, SM, VM, VM, VM, VM, ANY, ANY, ANY, ANY, VM],
+        out_specs=(VM, VM) + (ANY,) * 8 + (VM, VM, VM),
         scratch_shapes=[
+            pltpu.VMEM((HEADS, DK + ROWS_R, DK), BF),
+            pltpu.VMEM((SEGS, PIECE, DK), BF),
             pltpu.VMEM((SEGS, DK + ROWS_R, DK), BF),
             pltpu.VMEM((SEGS, PIECE, DK), BF),
             pltpu.VMEM((SEGS, PIECE, DK), STATE),
@@ -601,27 +609,15 @@
             collective_id=0, has_side_effects=True, vmem_limit_bytes=LIMIT
         ),
         name="forward_scan",
-    )(er, bt, key_rows, value_rows, queries, grad_out, picked, readout)
-
-    own_allowed = lax.dynamic_slice(allowed, (lax.axis_index("ctx"), 0), (1, 2))
-    one = pl.BlockSpec((SEG, DK), lambda h: (0, h))
-    wide = pl.BlockSpec((NM, 2 * DK), lambda h: (0, h))
-    dq, dk, dv, gm, stats = pl.pallas_call(
-        attention_kernel,
-        grid=(HEADS,),
-        out_shape=(
-            shape(block, F32),
-            shape(block, F32),
-            shape(block, F32),
-            shape((NM, 2 * WIDE), BF),
-            shape((8 * HEADS, SEG), F32),
-        ),
-        in_specs=[SM] + [one] * 8 + [wide],
-        out_specs=(one,) * 3 + (wide, pl.BlockSpec((8, SEG), lambda h: (h, 0))),
-        compiler_params=pltpu.CompilerParams(vmem_limit_bytes=LIMIT),
-        name="attention",
-    )(own_allowed, queries, grad_out, key_rows, value_rows, k1, v1, k2, v2, tok)
-
+    )(
+        retain, learn_rate, queries, key_rows, targets, positions,
+        key_rows, value_rows, queries, grad_out, readout,
+    )
+
+    segment = lax.axis_index("ctx")
+    row = lax.dynamic_slice(allowed, (segment, 0), (1, 2))
+    reach = lax.broadcasted_iota(jnp.int32, (1, 2), 1) < segment
+    bias = jnp.where((row == 1) & reach, 0.0, NEG).astype(F32)
     results = (
         shape(block, F32),
         shape(block, F32),
@@ -632,14 +628,20 @@
     outs = pl.pallas_call(
         backward_kernel,
         out_shape=results,
-        in_specs=[SM] + [VM] * 6 + [ANY] * 12,
+        in_specs=[SM, SM] + [VM] * 5 + [ANY] * 15,
         out_specs=(VM,) * 5,
         scratch_shapes=[
+            pltpu.VMEM(block, BF),
+        ] * 12
+        + [
+            pltpu.VMEM((SEGS, PIECE, DK), BF),
             pltpu.VMEM((SEGS, DK + ROWS_R, DK), BF),
-            pltpu.VMEM((SEGS, PIECE, DK), BF),
+            pltpu.VMEM(block, BF),
+            pltpu.VMEM((NM, 2 * WIDE), BF),
+            pltpu.VMEM((8 * HEADS, SEG), F32),
+            pltpu.VMEM((HEADS, SEG, 3 * SEG + NM), BF),
+            pltpu.VMEM((HEADS, SEG, SEG), BF),
         ]
-        + [pltpu.VMEM(block, BF)] * 7
-        + [pltpu.VMEM(block, F32)] * 3
         + [pltpu.VMEM((PEERS, NM, FH // PEERS), F32)]
         + sums
         + [
@@ -656,23 +658,23 @@
             pltpu.VMEM((2, 8 * HEADS, SEG), F32),
             pltpu.VMEM((PIECE, DK), F32),
             dma(SEGS), dma(SEGS), dma(SEGS), dma(SEGS), dma(SEGS // 2), dma(SEGS // 2),
-            dma(2 * PEERS), dma(2 * PEERS), dma(PEERS), dma(PEERS), dma(2), dma(2), dma(3), dma(12),
+            dma(2 * PEERS), dma(2 * PEERS), dma(PEERS), dma(PEERS), dma(2), dma(2), dma(3), dma(15),
         ],
         compiler_params=pltpu.CompilerParams(
             collective_id=1, has_side_effects=True, vmem_limit_bytes=LIMIT
         ),
         name="backward_scan",
     )(
-        learn_rate, gm, readout, picked, hid, positions, stats, er_all, mt, key_rows, value_rows, targets,
-        q1, g1, q2, g2, dq, dk, dv,
+        learn_rate, bias, tok, readout, picked, hid, positions,
+        queries, grad_out, key_rows, value_rows, k1, v1, k2, v2, q1, g1, q2, g2, mt, er_all, targets,
     )
     specs = (
-        (one,) * 3
-        + (pl.BlockSpec((SEG // HEADS, FH // PEERS), lambda h: (h, 0)),)
-        + (pl.BlockSpec((FH // SEGS, 2 * DK), lambda h: (0, h)),)
+        (pl.BlockSpec((SEG // 4, WIDE), lambda i: (i, 0)),) * 3
+        + (pl.BlockSpec((SEG // 4, FH // PEERS), lambda i: (i, 0)),)
+        + (pl.BlockSpec((FH // SEGS, 2 * DK), lambda i: (0, i)),)
     )
     return pl.pallas_call(
-        finish_kernel, grid=(HEADS,), out_shape=results, in_specs=list(specs), out_specs=specs, name="finish"
+        finish_kernel, grid=(4,), out_shape=results, in_specs=list(specs), out_specs=specs, name="finish"
     )(*outs)
 
 

time: 157 us -> 145 us (0.924)
  Pallas kernels: 154 us -> 143 us
    pallas_call x4 -> x2, Pallas kernels: 83.6 us -> 68.5 us  [the longest x1 64.2 us: on_device(): pl.pallas_call(backward_kernel, out_shape=results, in_specs=[SM, SM] + [V...]
    pallas_call x1, Pallas kernels: 70.7 us -> 74.5 us  [on_device(): pl.pallas_call(forward_kernel, out_shape=(shape((SEGS, DK + ROWS_R, DK),...]
where the time goes in v3:
time: 145 us
  Pallas kernels  143 us (99%)
    pallas_call x1, Pallas kernels, on_device(): pl.pallas_call(forward_kernel, out_shape=(shape((SEGS, DK + ROWS_R, DK),...  74.5 us
    pallas_call x1, Pallas kernels, on_device(): pl.pallas_call(backward_kernel, out_shape=results, in_specs=[SM, SM] + [V...  64.2 us
    pallas_call x1, Pallas kernels, on_device(): pl.pallas_call(finish_kernel, grid=(4,), out_shape=results, in_specs=list...  4.28 us

profile of v3, /device:TPU:0, one launch (start us, length us, event | category | flops | bytes accessed | tf_op | source)
XLA Modules:
  0.0 145.1 jit_solution(609703686144100615)
XLA Ops:
  0.6 0.0 copy-start
  0.7 0.7 copy-done
  1.3 0.1 constant_dynamic-slice_fusion
  1.4 0.1 copy.16
  1.5 0.5 and_select_fusion.bias
  2.0 74.5 %forward_scan.1 = (bf16[32,144,128]{2,1,0:T(8,128)(2,1)}, bf16[32,64,128]{2,1,0:T(8,128)(2,1)}, bf16[512,512]{1,0:T(8,128)(2,1)}, bf16[512,512]{1,0:T(8,128)(2,1...) custom-call(f32[1,4]{1,0:T(1,128)} %retain.1, ...), custom_call_target="tpu_custom_call" | custom-call | tf_op jit(solution)/shard_map/forward_scan/pallas_call | solution.py:579
  76.5 64.2 %backward_scan.1 = (f32[512,512]{1,0:T(8,128)}, f32[512,512]{1,0:T(8,128)}, f32[512,512]{1,0:T(8,128)}, f32[512,128]{1,0:T(8,128)}, f32[16,1024]{1,0:T(8,128)}) custom-call(f32[1,4]{1,0:T(1,128)} %rate.3, f32[1,2]{1,0:T(1,128)} %and_select_fusion.bias, bf16[128,1024]{1,0:T(8,128)(2,1)} %get-tuple-element.23.tok, bf16[512,1024]{1,0:T(8,128)(2,1)} %readout.3, ...), custom_call_target="tpu_custom_call" | custom-call | tf_op jit(solution)/shard_map/backward_scan/pallas_call | solution.py:628
  140.7 4.3 %finish.1 = (f32[512,512]{1,0:T(8,128)}, f32[512,512]{1,0:T(8,128)}, f32[512,512]{1,0:T(8,128)}, f32[512,128]{1,0:T(8,128)}, f32[16,1024]{1,0:T(8,128)}) custom-call(f32[512,512]{1,0:T(8,128)} %get-tuple-element.36.refs_0_, f32[512,512]{1,0:T(8,128)} %get-tuple-element.37.refs_1_, f32[512,512]{1,0:T(8,128)} %get-tuple-element.38.refs_2_, ...), custom_call_target="tpu_custom_call" | custom-call | tf_op jit(solution)/shard_map/finish/pallas_call | solution.py:676
Async XLA Ops:
  0.6 0.7 copy-start

commit v4 on v3

--- a/solution.py
+++ b/solution.py
@@ -145,17 +145,28 @@
     return started, summed, finished
 
 
-def forward_kernel(
-    retain, rate, q, k, z, pos, kk, vv, qq, gg, readout,
-    er_out, mt_out, k1, v1, k2, v2, q1, g1, q2, g2, hid, tok, picked,
-    er, bt, er_all, bt_all, outb, mt, mine_y, land_y, gath_y, part, state,
-    s_er, r_er, s_bt, r_bt, s_m, r_m, s_halo, r_halo, s_y, r_y, s_z, r_z, loc,
+def whole_kernel(
+    retain, rate, bias, qq, kk, zz, pos, v_h, g_h, readout_h,
+    out_q, out_k, out_v, out_z, out_r,
+    vv, gg, k1, v1, k2, v2, q1, g1, q2, g2, readout,
+    er, bt, picked, hid, tok, er_all, bt_all, outb, landed, mt,
+    mine_y, land_y, gath_y, mine_w, land_w, gath_w, part, state,
+    gm, stats, scores_grad, own_probs, gsb, gs_all, gout, gt, rterm, rlow, rpair, rbuf, rall, tparts, st_in,
+    s_er, r_er, s_bt, r_bt, s_m, r_m, s_halo, r_halo, s_y, r_y, s_z, r_z,
+    s_gs, r_gs, s_g, r_g, s_r, r_r, s_w, r_w, s_t, r_t, s_st, r_st, loc, fetch,
 ):
     me, my = lax.axis_index("ctx"), lax.axis_index("head")
     mz, mx, core = place(me)
     partner = me + 1 - 2 * core
+    scale = DK**-0.5
     entered = greet(me, my)
-    local_maps(retain, rate, q, k, z, pos, er, bt, picked)
+    fetched = [
+        pltpu.make_async_copy(src, dst, fetch.at[i])
+        for i, (src, dst) in enumerate(((v_h, vv), (g_h, gg), (readout_h, readout)))
+    ]
+    for copy in fetched:
+        copy.start()
+    local_maps(retain, rate, qq, kk, zz, pos, er, bt, picked)
     entered()
 
     def er_copy(x, to_x):
@@ -181,7 +192,7 @@
         return remote(bt.at[slot(to)], bt_all.at[src], s_bt.at[to], r_bt.at[src], {"ctx": to})
 
     def m_copy(to, src):
-        return remote(outb.at[to], mt.at[slot(src)], s_m.at[to], r_m.at[src], {"ctx": to})
+        return remote(outb.at[to], landed.at[slot(src)], s_m.at[to], r_m.at[src], {"ctx": to})
 
     for d in range(1, 4):
         er_copy(mx, lax.rem(mx + d, 4)).start()
@@ -208,8 +219,6 @@
     rows_near = [halo(gg, g1, 5, partner), halo(qq, q1, 7, partner)]
     keys_relay = [halo(v2, v1, 4, partner), halo(k2, k1, 6, partner)]
     rows_relay = [halo(g2, g1, 5, partner), halo(q2, q1, 7, partner)]
-    for copy in far[:2]:
-        copy.start()
 
     def relay(i):
         far[2 * i].wait_recv()
@@ -234,6 +243,15 @@
         over_z(d).wait_recv()
         over_core(d, core).start()
 
+    @pl.loop(1, SEGS)
+    def _(d):
+        bt_copy(lax.rem(me + d, SEGS), me).wait_send()
+
+    for copy in fetched:
+        copy.wait()
+    for copy in far[:2]:
+        copy.start()
+
     @pl.when(core == 0)
     def _():
         for copy in keys_near:
@@ -260,32 +278,30 @@
         outb[t] = old.astype(outb.dtype)
         state[...] = step(old, er_all, t, bt_all[t])
 
-        @pl.when((t > 0) & (t - 1 != me))
-        def _():
-            m_copy(t - 1, me).start()
-
-    @pl.when(me != SEGS - 1)
-    def _():
-        m_copy(SEGS - 1, me).start()
-
-    own_m = pltpu.make_async_copy(outb.at[me], mt.at[slot(me)], loc.at[2])
+    @pl.loop(1, SEGS)
+    def _(d):
+        m_copy(lax.rem(me + d, SEGS), me).start()
+
+    own_m = pltpu.make_async_copy(outb.at[me], landed.at[slot(me)], loc.at[2])
     own_m.start()
-    er_out[...] = er_all[...]
     own_m.wait()
 
     @pl.loop(1, SEGS)
     def _(d):
-        to = lax.rem(me + d, SEGS)
-        bt_copy(to, me).wait_send()
-        m_copy(to, me).wait_send()
-        m_copy(to, to).wait_recv()
+        m_copy(lax.rem(me + d, SEGS), me).wait_send()
 
     for copy in far[2:]:
         copy.start()
+
+    @pl.loop(1, SEGS)
+    def _(d):
+        src = lax.rem(me + d, SEGS)
+        m_copy(src, src).wait_recv()
+
     for h in range(HEADS):
-        m_h = mt[h * COLS : (h + 1) * COLS].reshape(FH, DK)
+        m_h = landed[h * COLS : (h + 1) * COLS].reshape(FH, DK)
         high = m_h.astype(BF)
-        mt_out[h * COLS : (h + 1) * COLS] = high.reshape(COLS, PIECE, DK)
+        mt[h * COLS : (h + 1) * COLS] = high.reshape(COLS, PIECE, DK)
         term = nt(picked[:, head(h)], high)
         if STATE == F32:
             term += nt(picked[:, head(h)], (m_h - high.astype(F32)).astype(BF))
@@ -298,46 +314,12 @@
     started()
     relay(0)
     summed()
+    relay(1)
     low = finished()
     hid[...] = low
     tok[...] = nn(low, readout[...]).astype(BF)
-    relay(1)
-    for d in range(1, 4):
-        er_copy(mx, lax.rem(mx + d, 4)).wait_send()
-        over_z(d).wait_send()
-    for d in range(4):
-        over_core(d, core).wait_send()
-    for copy in far:
-        copy.wait_send()
-    for copy in keys_near + rows_near:
-        copy.wait()
-
-
-def backward_kernel(
-    rate, bias, tok, readout, picked, hid, pos,
-    q_h, g_h, k_h, v_h, k1_h, v1_h, k2_h, v2_h, q1_h, g1_h, q2_h, g2_h, mt_h, er_all_h, zz_h,
-    out_q, out_k, out_v, out_z, out_r,
-    qq, gg, kk, vv, k1, v1, k2, v2, q1, g1, q2, g2, mt, er_all, zz,
-    gm, stats, scores_grad, own_probs,
-    part, mine_y, land_y, gath_y, gsb, gs_all, gout, gt, rterm, rlow, rpair, rbuf, rall, tparts, st_in, state,
-    s_gs, r_gs, s_g, r_g, s_r, r_r, s_y, r_y, s_t, r_t, s_st, r_st, loc, fetch,
-):
-    me, my = lax.axis_index("ctx"), lax.axis_index("head")
-    scale = DK**-0.5
-    entered = greet(me, my)
-    fetched = [
-        pltpu.make_async_copy(src, dst, fetch.at[i])
-        for i, (src, dst) in enumerate(
-            (
-                (q_h, qq), (k_h, kk), (k1_h, k1), (k2_h, k2), (v_h, vv), (v1_h, v1), (v2_h, v2), (g_h, gg),
-                (q1_h, q1), (g1_h, g1), (q2_h, q2), (g2_h, g2), (mt_h, mt), (er_all_h, er_all), (zz_h, zz),
-            )
-        )
-    ]
-    for copy in fetched:
-        copy.start()
-    for copy in fetched[:8]:
-        copy.wait()
+    for copy in keys_near:
+        copy.wait_recv()
 
     @pl.loop(0, HEADS)
     def _(h):
@@ -378,8 +360,6 @@
         )
         stats[pl.ds(pl.multiple_of(h * 8, 8), 8), :] = columns.T[0:8, :]
 
-    entered()
-
     def stat_copy(o):
         to = lax.rem(me + SEGS - o, SEGS)
         return remote(stats, st_in.at[o - 1], s_st.at[o - 1], r_st.at[o - 1], {"ctx": to})
@@ -390,9 +370,8 @@
     def g_copy(to, src):
         return remote(gout.at[to], gt.at[slot(src)], s_g.at[to], r_g.at[src], {"ctx": to})
 
-    core = lax.rem(me, 2)
     chip = lax.div(me, 2)
-    pair = remote(rlow.at[1 - core], rpair, s_r.at[0], r_r.at[0], {"ctx": me + 1 - 2 * core})
+    pair = remote(rlow.at[1 - core], rpair, s_r.at[0], r_r.at[0], {"ctx": partner})
 
     def r_copy(d):
         to = lax.rem(chip + d, SEGS // 2)
@@ -422,7 +401,7 @@
     term = nt(gm[...], readout[...])
     for j in range(PEERS):
         part[j] = term[:, head(j)]
-    started, summed, finished = sum_over_heads(lambda j: part[j], mine_y, land_y, gath_y, my, s_y, r_y)
+    started, summed, finished = sum_over_heads(lambda j: part[j], mine_w, land_w, gath_w, my, s_w, r_w)
     started()
     for o in (1, 2):
         stat_copy(o).start()
@@ -447,12 +426,12 @@
     def _(d):
         gs_copy(lax.rem(me + d, SEGS), me).start()
 
-    own_gs = pltpu.make_async_copy(gsb.at[slot(me)], gs_all.at[me], loc.at[0])
+    own_gs = pltpu.make_async_copy(gsb.at[slot(me)], gs_all.at[me], loc.at[3])
     own_gs.start()
     for o in (1, 2):
         stat_copy(o).wait()
-    for copy in fetched[8:]:
-        copy.wait()
+    for copy in rows_near:
+        copy.wait_recv()
     far_tile(1, 0)
     far_tile(2, 0)
     pair.wait()
@@ -463,7 +442,7 @@
     def _(d):
         r_copy(d).start()
 
-    own_r = pltpu.make_async_copy(rbuf.at[chip], rall.at[chip], loc.at[1])
+    own_r = pltpu.make_async_copy(rbuf.at[chip], rall.at[chip], loc.at[4])
     own_r.start()
     far_tile(2, 1)
     far_tile(1, 2)
@@ -486,15 +465,11 @@
         gout[t] = old.astype(BF)
         state[...] = step(old, er_all, t, gs_all[t])
 
-        @pl.when((i > 0) & (t + 1 != me))
-        def _():
-            g_copy(t + 1, me).start()
-
-    @pl.when(me != 0)
-    def _():
-        g_copy(0, me).start()
-
-    own_g = pltpu.make_async_copy(gout.at[me], gt.at[slot(me)], loc.at[2])
+    @pl.loop(1, SEGS)
+    def _(d):
+        g_copy(lax.rem(me + d, SEGS), me).start()
+
+    own_g = pltpu.make_async_copy(gout.at[me], gt.at[slot(me)], loc.at[5])
     own_g.start()
     far_tile(1, 3)
     far_tile(2, 3)
@@ -551,12 +526,36 @@
     for d in range(1, PEERS):
         grad += tparts[PEERS + d].astype(F32)
     out_z[...] = grad
+    for d in range(1, 4):
+        er_copy(mx, lax.rem(mx + d, 4)).wait_send()
+        over_z(d).wait_send()
+    for d in range(4):
+        over_core(d, core).wait_send()
+    for copy in far + keys_near + rows_near:
+        copy.wait_send()
 
 
 def finish_kernel(*refs):
-    half = len(refs) // 2
-    for src, dst in zip(refs[:half], refs[half:]):
-        dst[...] = src[...]
+    count = len(refs) // 3
+    arrays, (load, store) = refs[: 2 * count], refs[3 * count :]
+    held = refs[2 * count : 3 * count]
+    loads, stores = [], []
+    for i in range(count):
+        half = arrays[i].shape[0] // 2
+        for part in range(2):
+            rows = pl.ds(part * half, half)
+            slot_of = 2 * i + part
+            loads.append(pltpu.make_async_copy(arrays[i].at[rows], held[i].at[rows], load.at[slot_of]))
+            stores.append(
+                pltpu.make_async_copy(held[i].at[rows], arrays[count + i].at[rows], store.at[slot_of])
+            )
+    for copy in loads:
+        copy.start()
+    for first, then in zip(loads, stores):
+        first.wait()
+        then.start()
+    for copy in stores:
+        copy.wait()
 
 
 def shape(dims, kind):
@@ -571,49 +570,6 @@
     queries, key_rows, value_rows, targets, readout, retain, learn_rate, allowed, positions, grad_out
 ):
     block = (SEG, WIDE)
-    sums = [
-        pltpu.VMEM((PEERS, NM, FH // PEERS), F32),
-        pltpu.VMEM((PEERS, NM, FH // PEERS), F32),
-        pltpu.VMEM((PEERS, NM, FH // PEERS), BF),
-    ]
-    er_all, mt, k1, v1, k2, v2, q1, g1, q2, g2, hid, tok, picked = pl.pallas_call(
-        forward_kernel,
-        out_shape=(
-            shape((SEGS, DK + ROWS_R, DK), BF),
-            shape((SEGS, PIECE, DK), BF),
-        )
-        + (shape(block, BF),) * 8
-        + (
-            shape((NM, FH), BF),
-            shape((NM, 2 * WIDE), BF),
-            shape((NM, WIDE), BF),
-        ),
-        in_specs=[SM, SM, VM, VM, VM, VM, ANY, ANY, ANY, ANY, VM],
-        out_specs=(VM, VM) + (ANY,) * 8 + (VM, VM, VM),
-        scratch_shapes=[
-            pltpu.VMEM((HEADS, DK + ROWS_R, DK), BF),
-            pltpu.VMEM((SEGS, PIECE, DK), BF),
-            pltpu.VMEM((SEGS, DK + ROWS_R, DK), BF),
-            pltpu.VMEM((SEGS, PIECE, DK), BF),
-            pltpu.VMEM((SEGS, PIECE, DK), STATE),
-            pltpu.VMEM((SEGS, PIECE, DK), STATE),
-        ]
-        + sums
-        + [
-            pltpu.VMEM((PEERS, NM, FH // PEERS), F32),
-            pltpu.VMEM((PIECE, DK), F32),
-            dma(4), dma(4), dma(SEGS), dma(SEGS), dma(SEGS), dma(SEGS),
-            dma(8), dma(8), dma(2 * PEERS), dma(2 * PEERS), dma(8), dma(8), dma(3),
-        ],
-        compiler_params=pltpu.CompilerParams(
-            collective_id=0, has_side_effects=True, vmem_limit_bytes=LIMIT
-        ),
-        name="forward_scan",
-    )(
-        retain, learn_rate, queries, key_rows, targets, positions,
-        key_rows, value_rows, queries, grad_out, readout,
-    )
-
     segment = lax.axis_index("ctx")
     row = lax.dynamic_slice(allowed, (segment, 0), (1, 2))
     reach = lax.broadcasted_iota(jnp.int32, (1, 2), 1) < segment
@@ -625,56 +581,72 @@
         shape((SEG, FH // PEERS), F32),
         shape((FH // SEGS, 2 * WIDE), F32),
     )
+    sums = [
+        pltpu.VMEM((PEERS, NM, FH // PEERS), F32),
+        pltpu.VMEM((PEERS, NM, FH // PEERS), F32),
+        pltpu.VMEM((PEERS, NM, FH // PEERS), BF),
+    ]
+    low_pieces = pltpu.VMEM((SEGS, PIECE, DK), BF)
+    terms = (SEGS // 2, FH // SEGS, 2 * WIDE)
     outs = pl.pallas_call(
-        backward_kernel,
+        whole_kernel,
         out_shape=results,
-        in_specs=[SM, SM] + [VM] * 5 + [ANY] * 15,
+        in_specs=[SM, SM, SM] + [VM] * 4 + [ANY] * 3,
         out_specs=(VM,) * 5,
-        scratch_shapes=[
-            pltpu.VMEM(block, BF),
-        ] * 12
+        scratch_shapes=[pltpu.VMEM(block, BF)] * 10
         + [
-            pltpu.VMEM((SEGS, PIECE, DK), BF),
+            pltpu.VMEM((FH, 2 * WIDE), BF),
+            pltpu.VMEM((HEADS, DK + ROWS_R, DK), BF),
+            low_pieces,
+            pltpu.VMEM((NM, WIDE), BF),
+            pltpu.VMEM((NM, FH), BF),
+            pltpu.VMEM((NM, 2 * WIDE), BF),
             pltpu.VMEM((SEGS, DK + ROWS_R, DK), BF),
-            pltpu.VMEM(block, BF),
+            low_pieces,
+            pltpu.VMEM((SEGS, PIECE, DK), STATE),
+            pltpu.VMEM((SEGS, PIECE, DK), STATE),
+            low_pieces,
+        ]
+        + sums
+        + sums
+        + [
+            pltpu.VMEM((PEERS, NM, FH // PEERS), F32),
+            pltpu.VMEM((PIECE, DK), F32),
             pltpu.VMEM((NM, 2 * WIDE), BF),
             pltpu.VMEM((8 * HEADS, SEG), F32),
             pltpu.VMEM((HEADS, SEG, 3 * SEG + NM), BF),
             pltpu.VMEM((HEADS, SEG, SEG), BF),
-        ]
-        + [pltpu.VMEM((PEERS, NM, FH // PEERS), F32)]
-        + sums
-        + [
-            pltpu.VMEM((SEGS, PIECE, DK), BF),
-            pltpu.VMEM((SEGS, PIECE, DK), BF),
-            pltpu.VMEM((SEGS, PIECE, DK), BF),
-            pltpu.VMEM((SEGS, PIECE, DK), BF),
-            pltpu.VMEM((2, SEGS // 2, FH // SEGS, 2 * WIDE), F32),
-            pltpu.VMEM((2, SEGS // 2, FH // SEGS, 2 * WIDE), BF),
-            pltpu.VMEM((SEGS // 2, FH // SEGS, 2 * WIDE), BF),
-            pltpu.VMEM((SEGS // 2, FH // SEGS, 2 * WIDE), BF),
-            pltpu.VMEM((SEGS // 2, FH // SEGS, 2 * WIDE), BF),
+            low_pieces,
+            low_pieces,
+            low_pieces,
+            low_pieces,
+            pltpu.VMEM((2,) + terms, F32),
+            pltpu.VMEM((2,) + terms, BF),
+            pltpu.VMEM(terms, BF),
+            pltpu.VMEM(terms, BF),
+            pltpu.VMEM(terms, BF),
             pltpu.VMEM((2 * PEERS, SEG, FH // PEERS), BF),
             pltpu.VMEM((2, 8 * HEADS, SEG), F32),
-            pltpu.VMEM((PIECE, DK), F32),
+            dma(4), dma(4), dma(SEGS), dma(SEGS), dma(SEGS), dma(SEGS),
+            dma(8), dma(8), dma(2 * PEERS), dma(2 * PEERS), dma(8), dma(8),
             dma(SEGS), dma(SEGS), dma(SEGS), dma(SEGS), dma(SEGS // 2), dma(SEGS // 2),
-            dma(2 * PEERS), dma(2 * PEERS), dma(PEERS), dma(PEERS), dma(2), dma(2), dma(3), dma(15),
+            dma(2 * PEERS), dma(2 * PEERS), dma(PEERS), dma(PEERS), dma(2), dma(2), dma(6), dma(3),
         ],
         compiler_params=pltpu.CompilerParams(
-            collective_id=1, has_side_effects=True, vmem_limit_bytes=LIMIT
+            collective_id=0, has_side_effects=True, vmem_limit_bytes=LIMIT
         ),
-        name="backward_scan",
+        name="whole",
     )(
-        learn_rate, bias, tok, readout, picked, hid, positions,
-        queries, grad_out, key_rows, value_rows, k1, v1, k2, v2, q1, g1, q2, g2, mt, er_all, targets,
-    )
-    specs = (
-        (pl.BlockSpec((SEG // 4, WIDE), lambda i: (i, 0)),) * 3
-        + (pl.BlockSpec((SEG // 4, FH // PEERS), lambda i: (i, 0)),)
-        + (pl.BlockSpec((FH // SEGS, 2 * DK), lambda i: (0, i)),)
+        retain, learn_rate, bias, queries, key_rows, targets, positions, value_rows, grad_out, readout,
     )
     return pl.pallas_call(
-        finish_kernel, grid=(4,), out_shape=results, in_specs=list(specs), out_specs=specs, name="finish"
+        finish_kernel,
+        out_shape=results,
+        in_specs=[ANY] * 5,
+        out_specs=(ANY,) * 5,
+        scratch_shapes=[pltpu.VMEM(out.shape, F32) for out in results] + [dma(10), dma(10)],
+        compiler_params=pltpu.CompilerParams(vmem_limit_bytes=LIMIT),
+        name="finish",
     )(*outs)
 
 

time: 145 us -> 129 us (0.89)
  Pallas kernels: 143 us -> 126 us
    pallas_call x3 -> x2, Pallas kernels: 143 us -> 126 us  [the longest x1 123 us: on_device(): pl.pallas_call(whole_kernel, out_shape=results, in_specs=[SM, SM, SM] + [...]
where the time goes in v4:
time: 129 us; the launch traced here: 128 us
  Pallas kernels  126 us (98%)
    pallas_call x1, Pallas kernels, on_device(): pl.pallas_call(whole_kernel, out_shape=results, in_specs=[SM, SM, SM] + [...  123 us
    pallas_call x1, Pallas kernels, on_device(): pl.pallas_call(finish_kernel, out_shape=results, in_specs=[ANY] * 5, out_...  2.96 us

profile of v4, /device:TPU:0, one launch (start us, length us, event | category | flops | bytes accessed | tf_op | source)
XLA Modules:
  0.0 128.2 jit_solution(6121463326618012393)
XLA Ops:
  0.6 0.0 copy-start
  0.7 0.7 copy-done
  1.3 0.1 constant_dynamic-slice_fusion
  1.4 0.1 copy.16
  1.5 0.5 and_select_fusion.bias
  2.0 123.1 %whole.1 = (f32[512,512]{1,0:T(8,128)}, f32[512,512]{1,0:T(8,128)}, f32[512,512]{1,0:T(8,128)}, f32[512,128]{1,0:T(8,128)}, f32[16,1024]{1,0:T(8,128)}) custom-call(f32[1,4]{1,0:T(1,128)} %retain.1, f32[1,4]{1,0:T(1,128)} %rate.1, f32[1,2]{1,0:T(1,128)} %and_select_fusion.bias, bf16[512,512]{1,0:T(8,128)(2,1)} %qq.1, bf16[512,512]{1,0:T(8,128)(2,1)} %kk.1, ...), custom_call_target="tpu_custom_call" | custom-call | tf_op jit(solution)/shard_map/whole/pallas_call | solution.py:591
  125.1 3.0 %finish.1 = (f32[512,512]{1,0:T(8,128)}, f32[512,512]{1,0:T(8,128)}, f32[512,512]{1,0:T(8,128)}, f32[512,128]{1,0:T(8,128)}, f32[16,1024]{1,0:T(8,128)}) custom-call(f32[512,512]{1,0:T(8,128)} %get-tuple-element.10.refs_0_, f32[512,512]{1,0:T(8,128)} %get-tuple-element.11.refs_1_, f32[512,512]{1,0:T(8,128)} %get-tuple-element.12.refs_2_, ...), custom_call_target="tpu_custom_call" | custom-call | tf_op jit(solution)/shard_map/finish/pallas_call | solution.py:642
Async XLA Ops:
  0.6 0.7 copy-start

commit v5 on v4

--- a/solution.py
+++ b/solution.py
@@ -147,13 +147,13 @@
 
 def whole_kernel(
     retain, rate, bias, qq, kk, zz, pos, v_h, g_h, readout_h,
-    out_q, out_k, out_v, out_z, out_r,
-    vv, gg, k1, v1, k2, v2, q1, g1, q2, g2, readout,
+    ship_q, out_k, ship_v, out_z, out_r,
+    out_q, out_v, vv, gg, k1, v1, k2, v2, q1, g1, q2, g2, readout,
     er, bt, picked, hid, tok, er_all, bt_all, outb, landed, mt,
     mine_y, land_y, gath_y, mine_w, land_w, gath_w, part, state,
     gm, stats, scores_grad, own_probs, gsb, gs_all, gout, gt, rterm, rlow, rpair, rbuf, rall, tparts, st_in,
     s_er, r_er, s_bt, r_bt, s_m, r_m, s_halo, r_halo, s_y, r_y, s_z, r_z,
-    s_gs, r_gs, s_g, r_g, s_r, r_r, s_w, r_w, s_t, r_t, s_st, r_st, loc, fetch,
+    s_gs, r_gs, s_g, r_g, s_r, r_r, s_w, r_w, s_t, r_t, s_st, r_st, loc, fetch, ship,
 ):
     me, my = lax.axis_index("ctx"), lax.axis_index("head")
     mz, mx, core = place(me)
@@ -481,6 +481,12 @@
         m_h = mt[h * COLS : (h + 1) * COLS].reshape(FH, DK)
         grad_picked = nn(gh, m_h).astype(BF)
         out_q[:, head(h)] += nn(onehot, grad_picked)
+    shipped = [
+        pltpu.make_async_copy(out_v, ship_v, ship.at[0]),
+        pltpu.make_async_copy(out_q, ship_q, ship.at[1]),
+    ]
+    for copy in shipped:
+        copy.start()
 
     own_g.wait()
 
@@ -491,20 +497,19 @@
         g_copy(to, me).wait_send()
         g_copy(to, to).wait_recv()
 
-    term = jnp.zeros((SEG, FH), F32)
-    for h in range(HEADS):
-        g_h = gt[h * COLS : (h + 1) * COLS].reshape(FH, DK)
-        term += nt(kk[:, head(h)], g_h)
-    term = (term * (1.0 / SEG)).astype(BF)
-    for j in range(PEERS):
-        tparts[j] = term[:, head(j)]
-
     def t_copy(d):
         to = lax.rem(my + d, PEERS)
         return remote(tparts.at[to], tparts.at[PEERS + d], s_t.at[d], r_t.at[d], {"head": to})
 
-    for d in range(1, PEERS):
-        t_copy(d).start()
+    for d in (1, 2, 3, 0):
+        to = lax.rem(my + d, PEERS)
+        term = jnp.zeros((SEG, DK), F32)
+        for h in range(HEADS):
+            rows = gt[pl.ds(h * COLS + 2 * to, 2)].reshape(DK, DK)
+            term += nt(kk[:, head(h)], rows)
+        tparts[to] = (term * (1.0 / SEG)).astype(BF)
+        if d:
+            t_copy(d).start()
 
     for h in range(HEADS):
         g_h = gt[h * COLS : (h + 1) * COLS].reshape(FH, DK)
@@ -533,6 +538,8 @@
         over_core(d, core).wait_send()
     for copy in far + keys_near + rows_near:
         copy.wait_send()
+    for copy in shipped:
+        copy.wait()
 
 
 def finish_kernel(*refs):
@@ -592,8 +599,9 @@
         whole_kernel,
         out_shape=results,
         in_specs=[SM, SM, SM] + [VM] * 4 + [ANY] * 3,
-        out_specs=(VM,) * 5,
-        scratch_shapes=[pltpu.VMEM(block, BF)] * 10
+        out_specs=(ANY, VM, ANY, VM, VM),
+        scratch_shapes=[pltpu.VMEM(block, F32)] * 2
+        + [pltpu.VMEM(block, BF)] * 10
         + [
             pltpu.VMEM((FH, 2 * WIDE), BF),
             pltpu.VMEM((HEADS, DK + ROWS_R, DK), BF),
@@ -630,7 +638,7 @@
             dma(4), dma(4), dma(SEGS), dma(SEGS), dma(SEGS), dma(SEGS),
             dma(8), dma(8), dma(2 * PEERS), dma(2 * PEERS), dma(8), dma(8),
             dma(SEGS), dma(SEGS), dma(SEGS), dma(SEGS), dma(SEGS // 2), dma(SEGS // 2),
-            dma(2 * PEERS), dma(2 * PEERS), dma(PEERS), dma(PEERS), dma(2), dma(2), dma(6), dma(3),
+            dma(2 * PEERS), dma(2 * PEERS), dma(PEERS), dma(PEERS), dma(2), dma(2), dma(6), dma(3), dma(2),
         ],
         compiler_params=pltpu.CompilerParams(
             collective_id=0, has_side_effects=True, vmem_limit_bytes=LIMIT

time: 129 us -> 128 us (level)
  no operation moved by 1% of the time
where the time goes in v5:
time: 128 us; the launch traced here: 127 us
  Pallas kernels  125 us (98%)
    pallas_call x1, Pallas kernels, on_device(): pl.pallas_call(whole_kernel, out_shape=results, in_specs=[SM, SM, SM] + [...  122 us
    pallas_call x1, Pallas kernels, on_device(): pl.pallas_call(finish_kernel, out_shape=results, in_specs=[ANY] * 5, out_...  2.96 us

profile of v5, /device:TPU:0, one launch (start us, length us, event | category | flops | bytes accessed | tf_op | source)
XLA Modules:
  0.0 127.3 jit_solution(15298491682528486536)
XLA Ops:
  0.6 0.0 copy-start
  0.7 0.7 copy-done
  1.3 0.1 constant_dynamic-slice_fusion
  1.4 0.1 copy.16
  1.5 0.5 and_select_fusion.bias
  2.0 122.2 %whole.1 = (f32[512,512]{1,0:T(8,128)}, f32[512,512]{1,0:T(8,128)}, f32[512,512]{1,0:T(8,128)}, f32[512,128]{1,0:T(8,128)}, f32[16,1024]{1,0:T(8,128)}) custom-call(f32[1,4]{1,0:T(1,128)} %retain.1, f32[1,4]{1,0:T(1,128)} %rate.1, f32[1,2]{1,0:T(1,128)} %and_select_fusion.bias, bf16[512,512]{1,0:T(8,128)(2,1)} %qq.1, bf16[512,512]{1,0:T(8,128)(2,1)} %kk.1, ...), custom_call_target="tpu_custom_call" | custom-call | tf_op jit(solution)/shard_map/whole/pallas_call | solution.py:598
  124.2 3.0 %finish.1 = (f32[512,512]{1,0:T(8,128)}, f32[512,512]{1,0:T(8,128)}, f32[512,512]{1,0:T(8,128)}, f32[512,128]{1,0:T(8,128)}, f32[16,1024]{1,0:T(8,128)}) custom-call(f32[512,512]{1,0:T(8,128)} %get-tuple-element.10.refs_0_, f32[512,512]{1,0:T(8,128)} %get-tuple-element.11.refs_1_, f32[512,512]{1,0:T(8,128)} %get-tuple-element.12.refs_2_, ...), custom_call_target="tpu_custom_call" | custom-call | tf_op jit(solution)/shard_map/finish/pallas_call | solution.py:650
Async XLA Ops:
  0.6 0.7 copy-start
